TPU v7x, 128 devices: a whole 4x4x4 slice. The times are simulated.
128 devices in a mesh: section: 2 (over core), dp: 64 (over y, z, x).
Axes of the slice: x: 4, y: 4, z: 4, core: 2. Of those that a mesh axis runs over, the one named last changes fastest.
Arguments:
- inputs: bfloat16 [2, 4096, 960], P(None, 'dp'), may hold values from -16 to 16
- starts: int32 [2, 4096], P(None, 'dp'), may hold values from 0 to 64, as said below
- cotangent: bfloat16 [2, 4096, 960], P(None, 'dp'), may hold values from -16 to 16
- w_query: bfloat16 [2, 960, 960], P('section', 'dp'), may hold values from -0.1875 to 0.1875
- w_key: bfloat16 [2, 960, 320], P('section', 'dp'), may hold values from -0.1875 to 0.1875
- w_value: bfloat16 [2, 960, 320], P('section', 'dp'), may hold values from -0.1875 to 0.1875
- w_output: bfloat16 [2, 960, 960], P('section', 'dp'), may hold values from -0.75 to 0.75
- w_gate: bfloat16 [2, 960, 2560], P('section', 'dp'), may hold values from -0.1875 to 0.1875
- w_up: bfloat16 [2, 960, 2560], P('section', 'dp'), may hold values from -0.1875 to 0.1875
- w_down: bfloat16 [2, 2560, 960], P('section', 'dp'), may hold values from -0.15625 to 0.15625
- attn_gain: bfloat16 [2, 960], P('section', 'dp'), may hold values from 0.25 to 1.75
- ffn_gain: bfloat16 [2, 960], P('section', 'dp'), may hold values from 0.25 to 1.75
Outputs:
- activations: bfloat16 [2, 2, 4096, 960], P('section', None, 'dp')
- input_grads: bfloat16 [2, 2, 4096, 960], P('section', None, 'dp')
- grad_query: float32 [2, 960, 960], P('section', 'dp')
- grad_key: float32 [2, 960, 320], P('section', 'dp')
- grad_value: float32 [2, 960, 320], P('section', 'dp')
- grad_output: float32 [2, 960, 960], P('section', 'dp')
- grad_gate: float32 [2, 960, 2560], P('section', 'dp')
- grad_up: float32 [2, 960, 2560], P('section', 'dp')
- grad_down: float32 [2, 2560, 960], P('section', 'dp')
- grad_attn_gain: float32 [2, 960], P('section', 'dp')
- grad_ffn_gain: float32 [2, 960], P('section', 'dp')
Inputs may be any that keep to these rules, and one draw needn't show every extreme that they name: `starts`: within each aligned block of 64 rows (one index of dp, one micro-batch) sequences lie end to end from the block's first row, each row holding the block-local index of its sequence's first row; the rows after the last sequence are padding and hold 64. At least a quarter of every block's rows are in sequences, and some blocks are full.
All inputs are finite; a program needn't handle non-finite values.
Results may differ from a plain program's by a relative error of at most 0.023.
Values may be sent and summed in bfloat16 or wider, within the bound.
No kernel may reach another device: no remote copies, remote signals or barrier semaphores. Data moves between devices by JAX's collectives and lax.ppermute only.
A program may use at most 256 MiB of HBM per device.

v0:
```python
from functools import partial

import jax
import jax.numpy as jnp
from jax import lax
from jax.sharding import PartitionSpec as P

D = 960
HEADS = 15
KV_HEADS = 5
HEAD_DIM = 64
FF = 2560
QD = 960
KVD = 320


norm_eps = 1e-05
masked_score = -1e30
rope_base = 10000.0


def from_behind(value, axis, steps):
    count = lax.axis_size(axis)
    first, last = (max(0, -steps), min(count, count - steps))
    return lax.ppermute(value, axis, [(source, source + steps) for source in range(first, last)])


def rms_scale(values, gain):
    inverse = lax.rsqrt(jnp.mean(values * values, axis=-1, keepdims=True) + norm_eps)
    return values * inverse * gain


def rotate(values, cosine_table, sine_table):
    half_dim = values.shape[-1] // 2
    first_half = values[..., :half_dim]
    second_half = values[..., half_dim:]
    return jnp.concatenate(
        [
            first_half * cosine_table - second_half * sine_table,
            second_half * cosine_table + first_half * sine_table,
        ],
        axis=-1,
    )


def swiglu(gate_vals, up_vals):
    return jax.nn.silu(gate_vals) * up_vals


def right_trans(left, matrix):
    return lax.dot_general(
        left, matrix, (((1,), (1,)), ((), ())), preferred_element_type=jnp.float32
    )


def cross_rows(left, right):
    left_flat = left.reshape(-1, left.shape[-1])
    right_flat = right.reshape(-1, right.shape[-1])
    return lax.dot_general(
        left_flat, right_flat, (((0,), (0,)), ((), ())), preferred_element_type=jnp.float32
    )


def geometry(starts):
    row_count = starts.shape[0]
    local_rows = jnp.arange(row_count, dtype=jnp.int32)
    live_mask = starts <= local_rows
    position = jnp.where(live_mask, local_rows - starts, 0).astype(jnp.float32)
    frequency = rope_base ** (-2.0 * jnp.arange(HEAD_DIM // 2, dtype=jnp.float32) / HEAD_DIM)
    angles = position[:, None, None] * frequency[None, None, :]
    causal = local_rows[None, :] <= local_rows[:, None]
    inside = local_rows[None, :] >= starts[:, None]
    diagonal = local_rows[None, :] == local_rows[:, None]
    allowed = causal & inside | diagonal
    return (live_mask.astype(jnp.float32)[:, None], jnp.cos(angles), jnp.sin(angles), allowed)


def attention_block(normed_low, weights, cosine_table, sine_table, allowed):
    w_query, w_key, w_value = (weights[0], weights[1], weights[2])
    row_count = normed_low.shape[0]
    group_size = HEADS // KV_HEADS
    query_raw = jnp.dot(normed_low, w_query, preferred_element_type=jnp.float32)
    key_raw = jnp.dot(normed_low, w_key, preferred_element_type=jnp.float32)
    value_raw = jnp.dot(normed_low, w_value, preferred_element_type=jnp.float32)
    query_rot = rotate(
        query_raw.reshape(row_count, HEADS, HEAD_DIM), cosine_table, sine_table
    ).astype(jnp.bfloat16)
    key_rot = rotate(
        key_raw.reshape(row_count, KV_HEADS, HEAD_DIM), cosine_table, sine_table
    ).astype(jnp.bfloat16)
    value_heads = value_raw.astype(jnp.bfloat16).reshape(row_count, KV_HEADS, HEAD_DIM)
    grouped = query_rot.reshape(row_count, KV_HEADS, group_size, HEAD_DIM)
    scores = jnp.einsum(
        "qhgd,khd->hgqk", grouped, key_rot, preferred_element_type=jnp.float32
    ) * HEAD_DIM ** (-0.5)
    scores = jnp.where(allowed[None, None], scores, masked_score)
    row_peak = jnp.max(scores, axis=-1, keepdims=True)
    exp_scores = jnp.exp(scores - row_peak)
    probs_f32 = exp_scores / jnp.sum(exp_scores, axis=-1, keepdims=True)
    probs_low = probs_f32.astype(jnp.bfloat16)
    mixed_f32 = jnp.einsum(
        "hgqk,khd->qhgd", probs_low, value_heads, preferred_element_type=jnp.float32
    )
    mixed_low = mixed_f32.reshape(row_count, HEADS * HEAD_DIM).astype(jnp.bfloat16)
    return (mixed_low, (grouped, key_rot, value_heads, probs_f32, probs_low))


def layer_forward(source, weights, starts):
    w_query, w_key, w_value, w_output, w_gate, w_up, w_down, attn_gain, ffn_gain = weights
    live_rows, cosine_table, sine_table, allowed = geometry(starts)
    rows_f32 = source.astype(jnp.float32)
    normed_low = rms_scale(rows_f32, attn_gain.astype(jnp.float32)).astype(jnp.bfloat16)
    mixed_low, unused_saved = attention_block(
        normed_low, weights, cosine_table, sine_table, allowed
    )
    middle = rows_f32 + jnp.dot(mixed_low, w_output, preferred_element_type=jnp.float32)
    second_low = rms_scale(middle, ffn_gain.astype(jnp.float32)).astype(jnp.bfloat16)
    gate_vals = jnp.dot(second_low, w_gate, preferred_element_type=jnp.float32)
    up_vals = jnp.dot(second_low, w_up, preferred_element_type=jnp.float32)
    hidden_low = swiglu(gate_vals, up_vals).astype(jnp.bfloat16)
    result = (middle + jnp.dot(hidden_low, w_down, preferred_element_type=jnp.float32)) * live_rows
    return result.astype(jnp.bfloat16)


def layer_backward(source, weights, starts, upstream):
    w_query, w_key, w_value, w_output, w_gate, w_up, w_down, attn_gain, ffn_gain = weights
    live_rows, cosine_table, sine_table, allowed = geometry(starts)
    row_count = source.shape[0]
    group_size = HEADS // KV_HEADS
    score_scale = HEAD_DIM ** (-0.5)
    rows_f32 = source.astype(jnp.float32)
    first_normed, first_back = jax.vjp(rms_scale, rows_f32, attn_gain.astype(jnp.float32))
    normed_low = first_normed.astype(jnp.bfloat16)
    mixed_low, saved = attention_block(normed_low, weights, cosine_table, sine_table, allowed)
    grouped, key_rot, value_heads, probs_f32, probs_low = saved
    middle = rows_f32 + jnp.dot(mixed_low, w_output, preferred_element_type=jnp.float32)
    second_normed, second_back = jax.vjp(rms_scale, middle, ffn_gain.astype(jnp.float32))
    second_low = second_normed.astype(jnp.bfloat16)
    gate_vals = jnp.dot(second_low, w_gate, preferred_element_type=jnp.float32)
    up_vals = jnp.dot(second_low, w_up, preferred_element_type=jnp.float32)
    hidden_f32, hidden_back = jax.vjp(swiglu, gate_vals, up_vals)
    hidden_low = hidden_f32.astype(jnp.bfloat16)
    top_grad = upstream.astype(jnp.float32) * live_rows
    top_low = top_grad.astype(jnp.bfloat16)
    grad_hidden = right_trans(top_low, w_down)
    grad_gate_vals, grad_up_vals = hidden_back(grad_hidden)
    gate_low = grad_gate_vals.astype(jnp.bfloat16)
    up_low = grad_up_vals.astype(jnp.bfloat16)
    grad_second = right_trans(gate_low, w_gate) + right_trans(up_low, w_up)
    grad_middle_norm, grad_ffn_gain = second_back(grad_second)
    grad_middle = top_grad + grad_middle_norm
    middle_low = grad_middle.astype(jnp.bfloat16)
    grad_mixed = right_trans(middle_low, w_output).astype(jnp.bfloat16)
    grad_mixed = grad_mixed.reshape(row_count, KV_HEADS, group_size, HEAD_DIM)
    grad_probs = jnp.einsum(
        "qhgd,khd->hgqk", grad_mixed, value_heads, preferred_element_type=jnp.float32
    )
    grad_value_heads = jnp.einsum(
        "hgqk,qhgd->khd", probs_low, grad_mixed, preferred_element_type=jnp.float32
    )
    row_inner = jnp.sum(probs_f32 * grad_probs, axis=-1, keepdims=True)
    grad_scores = (probs_f32 * (grad_probs - row_inner)).astype(jnp.bfloat16)
    grad_query_rot = (
        jnp.einsum("hgqk,khd->qhgd", grad_scores, key_rot, preferred_element_type=jnp.float32)
        * score_scale
    )
    grad_key_rot = (
        jnp.einsum("hgqk,qhgd->khd", grad_scores, grouped, preferred_element_type=jnp.float32)
        * score_scale
    )
    grad_query_raw = rotate(
        grad_query_rot.reshape(row_count, HEADS, HEAD_DIM), cosine_table, -sine_table
    )
    grad_query_raw = grad_query_raw.reshape(row_count, HEADS * HEAD_DIM).astype(jnp.bfloat16)
    grad_key_raw = (
        rotate(grad_key_rot, cosine_table, -sine_table)
        .reshape(row_count, KV_HEADS * HEAD_DIM)
        .astype(jnp.bfloat16)
    )
    grad_value_raw = grad_value_heads.reshape(row_count, KV_HEADS * HEAD_DIM).astype(jnp.bfloat16)
    grad_normed = right_trans(grad_query_raw, w_query)
    grad_normed = grad_normed + right_trans(grad_key_raw, w_key)
    grad_normed = grad_normed + right_trans(grad_value_raw, w_value)
    grad_rows_norm, grad_attn_gain = first_back(grad_normed)
    grad_rows = grad_middle + grad_rows_norm
    operands = (
        normed_low,
        grad_query_raw,
        grad_key_raw,
        grad_value_raw,
        mixed_low,
        middle_low,
        second_low,
        gate_low,
        up_low,
        hidden_low,
        top_low,
    )
    return (grad_rows.astype(jnp.bfloat16), (grad_attn_gain, grad_ffn_gain), operands)


def weight_grads(operands):
    (
        normed_low,
        grad_query_raw,
        grad_key_raw,
        grad_value_raw,
        mixed_low,
        middle_low,
        second_low,
        gate_low,
        up_low,
        hidden_low,
        top_low,
    ) = operands
    return (
        cross_rows(normed_low, grad_query_raw),
        cross_rows(normed_low, grad_key_raw),
        cross_rows(normed_low, grad_value_raw),
        cross_rows(mixed_low, middle_low),
        cross_rows(second_low, gate_low),
        cross_rows(second_low, up_low),
        cross_rows(hidden_low, top_low),
    )


def flat_grads(grads, owner_count):
    pieces = [grad.reshape(owner_count, -1) for grad in grads]
    joined = jnp.concatenate(pieces, axis=1)
    width = joined.shape[1]
    padded = (width + 127) // 128 * 128
    return jnp.pad(joined, ((0, 0), (0, padded - width)))


def unflat_grads(flat_row, shard_shapes):
    flat_row = flat_row.reshape(-1)
    results = []
    offset = 0
    for shape in shard_shapes:
        length = 1
        for extent in shape:
            length = length * extent
        results.append(flat_row[offset : offset + length].reshape(shape))
        offset = offset + length
    return tuple(results)


def store_slot(buffer, rows_new, slot_idx, active):
    current = lax.dynamic_index_in_dim(buffer, slot_idx, 0, keepdims=False)
    chosen = jnp.where(active, rows_new, current)
    return lax.dynamic_update_index_in_dim(buffer, chosen, slot_idx, 0)


def body(
    inputs,
    starts,
    cotangent,
    w_query,
    w_key,
    w_value,
    w_output,
    w_gate,
    w_up,
    w_down,
    attn_gain,
    ffn_gain,
):
    section_idx = lax.axis_index("section")
    section_count = lax.axis_size("section")
    owner_count = lax.axis_size("dp")
    last_section = section_count - 1
    micro_count = inputs.shape[0]
    tick_count = micro_count + section_count - 1
    shard_list = (w_query, w_key, w_value, w_output, w_gate, w_up, w_down, attn_gain, ffn_gain)
    shard_shapes = tuple((piece.shape for piece in shard_list))
    gathered = (
        lax.all_gather(w_query, "dp", axis=1, tiled=True),
        lax.all_gather(w_key, "dp", axis=1, tiled=True),
        lax.all_gather(w_value, "dp", axis=1, tiled=True),
        lax.all_gather(w_output, "dp", axis=1, tiled=True),
        lax.all_gather(w_gate, "dp", axis=1, tiled=True),
        lax.all_gather(w_up, "dp", axis=1, tiled=True),
        lax.all_gather(w_down, "dp", axis=1, tiled=True),
        lax.all_gather(attn_gain, "dp", axis=1, tiled=True),
        lax.all_gather(ffn_gain, "dp", axis=1, tiled=True),
    )
    weights = tuple((piece[0] for piece in gathered))
    blank_rows = jnp.zeros(inputs.shape[1:], jnp.bfloat16)
    kept_in = jnp.zeros(inputs.shape, jnp.bfloat16)
    section_acts = jnp.zeros(inputs.shape, jnp.bfloat16)
    received = blank_rows
    for moment in range(tick_count):
        slot_raw = moment - section_idx
        active = (slot_raw >= 0) & (slot_raw < micro_count)
        slot_idx = jnp.clip(slot_raw, 0, micro_count - 1)
        feed_rows = jnp.where(section_idx == 0, inputs[min(moment, micro_count - 1)], received)
        starts_now = starts[slot_idx]
        produced = lax.cond(
            active, partial(layer_forward, feed_rows, weights, starts_now), lambda: blank_rows
        )
        kept_in = store_slot(kept_in, feed_rows, slot_idx, active)
        section_acts = store_slot(section_acts, produced, slot_idx, active)
        if moment + 1 < tick_count:
            received = from_behind(produced, "section", 1)
    regathered = (
        lax.all_gather(w_query, "dp", axis=1, tiled=True),
        lax.all_gather(w_key, "dp", axis=1, tiled=True),
        lax.all_gather(w_value, "dp", axis=1, tiled=True),
        lax.all_gather(w_output, "dp", axis=1, tiled=True),
        lax.all_gather(w_gate, "dp", axis=1, tiled=True),
        lax.all_gather(w_up, "dp", axis=1, tiled=True),
        lax.all_gather(w_down, "dp", axis=1, tiled=True),
        lax.all_gather(attn_gain, "dp", axis=1, tiled=True),
        lax.all_gather(ffn_gain, "dp", axis=1, tiled=True),
    )
    back_weights = tuple((piece[0] for piece in regathered))
    row_count = inputs.shape[1]
    operand_widths = (D, QD, KVD, KVD, QD, D, D, FF, FF, FF, D)
    blank_operands = tuple(
        (jnp.zeros((row_count, width), jnp.bfloat16) for width in operand_widths)
    )
    blank_gains = (
        jnp.zeros(back_weights[7].shape, jnp.float32),
        jnp.zeros(back_weights[8].shape, jnp.float32),
    )
    operand_store = tuple(
        (jnp.zeros((micro_count, row_count, width), jnp.bfloat16) for width in operand_widths)
    )
    gain_totals = blank_gains
    shard_totals = tuple((jnp.zeros(shape, jnp.float32) for shape in shard_shapes))
    input_grads = jnp.zeros(inputs.shape, jnp.bfloat16)
    returned = blank_rows
    for moment in range(tick_count):
        slot_raw = moment - (last_section - section_idx)
        active = (slot_raw >= 0) & (slot_raw < micro_count)
        slot_idx = jnp.clip(slot_raw, 0, micro_count - 1)
        upstream = jnp.where(
            section_idx == last_section, cotangent[min(moment, micro_count - 1)], returned
        )
        source = lax.dynamic_index_in_dim(kept_in, slot_idx, 0, keepdims=False)
        starts_now = starts[slot_idx]

        def run_keep():
            return layer_backward(source, back_weights, starts_now, upstream)

        def skip_keep():
            return (blank_rows, blank_gains, blank_operands)

        grad_rows, gain_grads, operands = lax.cond(active, run_keep, skip_keep)
        gain_totals = tuple(
            (old_sum + new_sum for old_sum, new_sum in zip(gain_totals, gain_grads))
        )
        operand_store = tuple(
            (
                store_slot(buffer, member, slot_idx, active)
                for buffer, member in zip(operand_store, operands)
            )
        )
        input_grads = store_slot(input_grads, grad_rows, slot_idx, active)
        if moment + 1 < tick_count:
            returned = from_behind(grad_rows, "section", -1)
    totals = weight_grads(operand_store) + gain_totals
    scattered = lax.psum_scatter(
        flat_grads(totals, owner_count), "dp", scatter_dimension=0, tiled=True
    )
    shard_totals = unflat_grads(scattered, shard_shapes)
    return (section_acts[None], input_grads[None]) + tuple(shard_totals)


def solution(mesh):
    return jax.shard_map(
        body,
        mesh=mesh,
        in_specs=(
            P(None, "dp", None),
            P(None, "dp"),
            P(None, "dp", None),
            P("section", "dp", None),
            P("section", "dp", None),
            P("section", "dp", None),
            P("section", "dp", None),
            P("section", "dp", None),
            P("section", "dp", None),
            P("section", "dp", None),
            P("section", "dp"),
            P("section", "dp"),
        ),
        out_specs=(
            P("section", None, "dp", None),
            P("section", None, "dp", None),
            P("section", "dp", None),
            P("section", "dp", None),
            P("section", "dp", None),
            P("section", "dp", None),
            P("section", "dp", None),
            P("section", "dp", None),
            P("section", "dp", None),
            P("section", "dp"),
            P("section", "dp"),
        ),
        check_vma=False,
    )
```

profile of v0, /device:TPU:0, one launch (start us, length us, event | category | flops | bytes accessed | tf_op | source)
XLA Modules:
  0.0 1488.5 jit_solution(15037251605952661277)
XLA Ops:
  15.2 188.1 %all_gather.37 = bf16[1,960,320]{2,0,1:T(2,128)(2,1)S(1)} all-gather(bf16[1,15,320]{2,0,1:T(2,128)(2,1)S(1)} %copy.462), channel_id=1, replica_groups=mesh['section'=2,'dp'=64] {'dp'}, dimensions={1}, use_global_device_ids=true | all-gather | bytes 624000 | tf_op jit(solution)/shard_map/all_gather | solution.py:279
  206.3 183.7 %all_gather.38 = bf16[1,960,320]{2,0,1:T(2,128)(2,1)S(1)} all-gather(bf16[1,15,320]{2,0,1:T(2,128)(2,1)S(1)} %copy.464), channel_id=1, replica_groups=mesh['section'=2,'dp'=64] {'dp'}, dimensions={1}, use_global_device_ids=true | all-gather | bytes 624000 | tf_op jit(solution)/shard_map/all_gather | solution.py:278
  394.3 173.6 %all-reduce.4 = (bf16[960]{0:T(1024)(128)(2,1)S(1)}, bf16[960]{0:T(1024)(128)(2,1)S(1)}) all-reduce(bf16[960]{0:T(1024)(128)(2,1)S(1)} %dynamic-update-slice, bf16[960]{0:T(1024)(128)(2,1)S(1)} %dynamic-update-slice.1), channel_id=1, replica_groups=mesh['section'=2,'dp'=64] {'dp'}, use_global_device_ids=true, to_apply=%add.1 | all-reduce | flops 1920 | bytes 7680 | tf_op jit(solution)/shard_map/squeeze | solution.py:287
  568.6 2.9 copy.614
  571.5 4.2 copy.613
  575.7 7.3 copy.612
  583.0 7.2 copy.611
  590.9 39.3 %conditional.6 = (bf16[64,960]{1,0:T(8,128)(2,1)}) conditional(s32[]{:T(128)} %convert_element_type.647, () %tuple.72, (pred[]{:T(512)}, bf16[1,64,960]{2,1,0:T(8,128)(2,1)}, bf16[64,960]{1,0:T(8,128)(2,1)}, bf16[960]{0:T(1024)(128)(2,1)S(1)}, bf16[960,320]{0,1:T(8,128)(2,1)S(1)}, /*index=5*/s32[2,64]{1,0:T(2,128)S(1)}, s32[]{:T(128)}, ...), branch_computations={%region_0.1_spmd, %region_1.6_spmd} | conditional | flops 1286292992 | bytes 26960564 | solution.py:298
  618.9 4.3 fusion.22
  623.2 6.9 fusion.9
  634.4 39.3 %conditional.7 = (bf16[64,960]{1,0:T(8,128)(2,1)}) conditional(s32[]{:T(128)} %convert_element_type.648, () %tuple.74, (bf16[64,960]{1,0:T(8,128)(2,1)}, bf16[960]{0:T(1024)(128)(2,1)S(1)}, bf16[960,320]{0,1:T(8,128)(2,1)S(1)}, s32[2,64]{1,0:T(2,128)S(1)}, s32[]{:T(128)}, /*index=5*/bf16[960,320]{0,1:T(8,128)(2,1)S(1)}, ...), branch_computations={%region_6.7_spmd, %region_7.12_spmd} | conditional | flops 1286231552 | bytes 26223256 | solution.py:298
  662.5 4.3 fusion.84
  666.8 6.9 fusion.71
  673.7 3.0 collective-permute-start.1
  680.6 9.7 conditional.9
  711.3 38.1 %collective-permute-done.2 = bf16[64,960]{1,0:T(8,128)(2,1)} collective-permute-done((bf16[64,960]{1,0:T(8,128)(2,1)}, bf16[64,960]{1,0:T(8,128)(2,1)}, u32[]{:S(2)}, u32[]{:S(2)}) %collective-permute-start.2) | collective-permute-done | bytes 122912 | tf_op jit(solution)/shard_map/ppermute | solution.py:25
  749.4 65.7 %conditional.10 = (bf16[64,960]{1,0:T(8,128)(2,1)}, f32[960]{0:T(1024)}, f32[960]{0:T(1024)}, bf16[64,960]{1,0:T(8,128)(2,1)}, bf16[64,320]{0,1:T(8,128)(2,1)}, ...) conditional(s32[]{:T(128)} %convert_element_type.651, () %tuple.80, ...), branch_computations={%region_29.30_spmd, %region_30.40_spmd} | conditional | flops 2275088896 | bytes 119995208 | solution.py:349
  758.5 2.6 copy.479
  776.3 3.8 fusion.371
  780.2 2.8 fusion.370
  783.0 3.0 multiply_convert_fusion.16
  788.7 3.3 multiply_reduce_fusion.8
  855.2 65.8 %conditional.11 = (bf16[64,960]{1,0:T(8,128)(2,1)}, f32[960]{0:T(1024)}, f32[960]{0:T(1024)}, bf16[64,960]{1,0:T(8,128)(2,1)}, bf16[64,320]{0,1:T(8,128)(2,1)}, ...) conditional(s32[]{:T(128)} %convert_element_type.652, () %tuple.82, ...), branch_computations={%region_40.41_spmd, %region_41.51_spmd} | conditional | flops 2275088896 | bytes 119995208 | solution.py:349
  882.0 3.8 fusion.375
  885.9 2.8 fusion.374
  888.7 2.9 multiply_convert_fusion.20
  894.3 3.3 multiply_reduce_fusion.12
  924.4 3.6 convolution_bitcast_fusion.13
  928.0 5.3 reshape.1296
  936.0 2.9 reshape.1297
  941.4 2.9 reshape.1298
  948.8 5.4 reshape.1299
  956.9 6.1 convolution_bitcast_fusion.11
  962.9 11.9 reshape.1300
  976.0 6.1 convolution_bitcast_fusion.10
  982.1 12.0 reshape.1301
  996.0 5.5 convolution_bitcast_fusion.9
  1001.6 12.2 reshape.1302
  1014.8 11.4 dynamic-update-slice.2
  1026.2 6.4 dynamic-update-slice.3
  1032.6 6.2 dynamic-update-slice.4
  1038.9 12.3 dynamic-update-slice.5
  1051.2 8.6 constant_dynamic-update-slice_fusion.8
  1059.8 4.3 constant_dynamic-update-slice_fusion.7
  1064.2 8.3 constant_dynamic-update-slice_fusion.6
  1075.3 27.2 %pad.4 = f32[64,153728]{1,0:T(8,128)} pad(f32[64,153630]{1,0:T(8,128)} %dynamic-update-slice.10, f32[]{:T(128)} %constant.520.clone.1), padding=0_0x0_98 | pad | bytes 78683648 | tf_op jit(solution)/shard_map/jit(_pad)/pad | solution.py:232
  1107.4 360.1 %all-reduce.7.cloned.1.call-done = f32[64,153728]{1,0:T(8,128)} async-done(((f32[64,153728]{1,0:T(8,128)}), f32[64,153728]{1,0:T(8,128)}) %all-reduce.7.cloned.1.call-update) | async-done | bytes 39354384
  1474.3 4.4 dynamic-slice_reduce_fusion
  (552 shorter events, 288.8 us)
Async XLA Ops:
  7.2 385.2 %copy-start.120 = (u32[128]{0:T(128)S(1)}, u32[128]{0:T(128)}, u32[]{:S(2)}) copy-start(u32[128]{0:T(128)} %constant.534) | copy-start | bytes 1540
  7.2 386.6 %copy-start.126 = (bf16[1,15]{1,0:T(2,128)(2,1)S(1)}, bf16[1,15]{1,0:T(2,128)(2,1)}, u32[]{:S(2)}) copy-start(bf16[1,15]{1,0:T(2,128)(2,1)} %param.34) | copy-start | bytes 94
  7.2 386.9 %copy-start.127 = (bf16[1,15]{1,0:T(2,128)(2,1)S(1)}, bf16[1,15]{1,0:T(2,128)(2,1)}, u32[]{:S(2)}) copy-start(bf16[1,15]{1,0:T(2,128)(2,1)} %param.35) | copy-start | bytes 94
  7.2 560.7 %copy-start.70 = (bf16[2,64,960]{2,1,0:T(8,128)(2,1)S(1)}, bf16[2,64,960]{2,1,0:T(8,128)(2,1)}, u32[]{:S(2)}) copy-start(bf16[2,64,960]{2,1,0:T(8,128)(2,1)} %param.24) | copy-start | bytes 737284
  7.2 561.4 %all-gather.6.cloned.1.call-start = ((), (), s32[]{:S(2)}) async-start(), calls=%async_computation | async-start | bytes 3993600 | tf_op jit(solution)/shard_map/all_gather | solution.py:277
  8.8 562.8 %all-gather.8.cloned.1.call-start = ((), (), s32[]{:S(2)}) async-start(), calls=%async_computation.1 | async-start | bytes 3993600 | tf_op jit(solution)/shard_map/all_gather | solution.py:280
  10.3 565.5 %all-gather.10.cloned.1.call-start = ((), (), s32[]{:S(2)}) async-start(), calls=%async_computation.2 | async-start | bytes 9984000 | tf_op jit(solution)/shard_map/all_gather | solution.py:281
  12.0 571.0 %all-gather.12.cloned.1.call-start = ((), (), s32[]{:S(2)}) async-start(), calls=%async_computation.3 | async-start | bytes 9984000 | tf_op jit(solution)/shard_map/all_gather | solution.py:282
  13.8 576.5 %all-gather.14.cloned.1.call-start = ((), (), s32[]{:S(2)}) async-start(), calls=%async_computation.4 | async-start | bytes 5324800 | tf_op jit(solution)/shard_map/all_gather | solution.py:283
  14.4 1453.1 %all-reduce.7.cloned.1.call-start = ((), (), s32[]{:S(2)}) async-start(), calls=%async_computation.5 | async-start | bytes 78708736
  205.6 474.4 %copy-start.4 = (bf16[1,960,320]{1,2,0:T(8,128)(2,1)}, bf16[1,960,320]{1,2,0:T(8,128)(2,1)S(1)}, u32[]{:S(2)}) copy-start(bf16[1,960,320]{1,2,0:T(8,128)(2,1)S(1)} %copy.463) | copy-start | bytes 1843204
  392.4 287.6 %copy-start.14 = (bf16[1,960,320]{1,2,0:T(8,128)(2,1)}, bf16[1,960,320]{1,2,0:T(8,128)(2,1)S(1)}, u32[]{:S(2)}) copy-start(bf16[1,960,320]{1,2,0:T(8,128)(2,1)S(1)} %copy.465) | copy-start | bytes 1843204
  567.9 112.1 %copy-start.94 = (bf16[960]{0:T(1024)(128)(2,1)}, bf16[960]{0:T(1024)(128)(2,1)S(1)}, u32[]{:S(2)}) copy-start(bf16[960]{0:T(1024)(128)(2,1)S(1)} %get-tuple-element.1183) | copy-start | bytes 5764
  567.9 112.1 %copy-start.98 = (bf16[960]{0:T(1024)(128)(2,1)}, bf16[960]{0:T(1024)(128)(2,1)S(1)}, u32[]{:S(2)}) copy-start(bf16[960]{0:T(1024)(128)(2,1)S(1)} %get-tuple-element.1184) | copy-start | bytes 5764
  630.2 2.6 collective-permute-start
  673.7 4.6 collective-permute-start.1
  690.3 59.0 %collective-permute-start.2 = (bf16[64,960]{1,0:T(8,128)(2,1)}, bf16[64,960]{1,0:T(8,128)(2,1)}, u32[]{:S(2)}, u32[]{:S(2)}) collective-permute-start(bf16[64,960]{1,0:T(8,128)(2,1)} %get-tuple-element.623), channel_id=1, source_target_pairs={{64,0},{65,1},{66,2},{67,3},{68,4},{69,5},{70,6},{71,7},{72,8},{73... | collective-permute-start | bytes 368648 | tf_op jit(solution)/shard_map/ppermute | solution.py:25
  695.3 54.0 %copy-start.5 = (bf16[1,960,320]{1,2,0:T(8,128)(2,1)S(1)}, bf16[1,960,320]{1,2,0:T(8,128)(2,1)}, u32[]{:S(2)}) copy-start(bf16[1,960,320]{1,2,0:T(8,128)(2,1)} %copy-done.4) | copy-start | bytes 1843204
  695.3 54.0 %copy-start.15 = (bf16[1,960,320]{1,2,0:T(8,128)(2,1)S(1)}, bf16[1,960,320]{1,2,0:T(8,128)(2,1)}, u32[]{:S(2)}) copy-start(bf16[1,960,320]{1,2,0:T(8,128)(2,1)} %copy-done.14) | copy-start | bytes 1843204
  695.3 54.0 %copy-start.95 = (bf16[960]{0:T(1024)(128)(2,1)S(1)}, bf16[960]{0:T(1024)(128)(2,1)}, u32[]{:S(2)}) copy-start(bf16[960]{0:T(1024)(128)(2,1)} %copy-done.94) | copy-start | bytes 5764
  695.3 54.0 %copy-start.108 = (s32[2,64]{1,0:T(2,128)S(1)}, s32[2,64]{1,0:T(2,128)}, u32[]{:S(2)}) copy-start(s32[2,64]{1,0:T(2,128)} %param.25) | copy-start | bytes 1540
  749.4 15.5 %copy-start.10 = (bf16[960,320]{0,1:T(8,128)(2,1)}, bf16[960,320]{0,1:T(8,128)(2,1)S(1)}, u32[]{:S(2)}) copy-start(bf16[960,320]{0,1:T(8,128)(2,1)S(1)} %get-tuple-element.1128) | copy-start | bytes 1843204 | tf_op jit(solution)/shard_map/cond
  749.4 15.5 %copy-start.20 = (bf16[960,320]{0,1:T(8,128)(2,1)}, bf16[960,320]{0,1:T(8,128)(2,1)S(1)}, u32[]{:S(2)}) copy-start(bf16[960,320]{0,1:T(8,128)(2,1)S(1)} %get-tuple-element.549) | copy-start | bytes 1843204 | tf_op jit(solution)/shard_map/cond
  767.8 12.4 slice-start.14
  815.1 40.1 %collective-permute-start.3 = (bf16[64,960]{1,0:T(8,128)(2,1)}, bf16[64,960]{1,0:T(8,128)(2,1)}, u32[]{:S(2)}, u32[]{:S(2)}) collective-permute-start(bf16[64,960]{1,0:T(8,128)(2,1)} %get-tuple-element.624), channel_id=1, source_target_pairs={{64,0},{65,1},{66,2},{67,3},{68,4},{69,5},{70,6},{71,7},{72,8},{73... | collective-permute-start | bytes 368648 | tf_op jit(solution)/shard_map/ppermute | solution.py:25
  818.2 37.0 %copy-start.6 = (bf16[1,960,320]{1,2,0:T(8,128)(2,1)S(1)}, bf16[1,960,320]{1,2,0:T(8,128)(2,1)}, u32[]{:S(2)}) copy-start(bf16[1,960,320]{1,2,0:T(8,128)(2,1)} %copy-done.4) | copy-start | bytes 1843204
  818.2 37.0 %copy-start.16 = (bf16[1,960,320]{1,2,0:T(8,128)(2,1)S(1)}, bf16[1,960,320]{1,2,0:T(8,128)(2,1)}, u32[]{:S(2)}) copy-start(bf16[1,960,320]{1,2,0:T(8,128)(2,1)} %copy-done.14) | copy-start | bytes 1843204
  818.2 37.0 %copy-start.96 = (bf16[960]{0:T(1024)(128)(2,1)S(1)}, bf16[960]{0:T(1024)(128)(2,1)}, u32[]{:S(2)}) copy-start(bf16[960]{0:T(1024)(128)(2,1)} %copy-done.94) | copy-start | bytes 5764
  818.2 37.0 %copy-start.109 = (s32[2,64]{1,0:T(2,128)S(1)}, s32[2,64]{1,0:T(2,128)}, u32[]{:S(2)}) copy-start(s32[2,64]{1,0:T(2,128)} %param.25) | copy-start | bytes 1540
  832.1 17.9 %copy-start.68 = (bf16[2,64,320]{2,1,0:T(8,128)(2,1)S(1)}, bf16[2,64,320]{2,1,0:T(8,128)(2,1)}, u32[]{:S(2)}) copy-start(bf16[2,64,320]{2,1,0:T(8,128)(2,1)} %constant_dynamic-update-slice_fusion.1) | copy-start | bytes 245764
  855.2 15.3 %copy-start.12 = (bf16[960,320]{0,1:T(8,128)(2,1)}, bf16[960,320]{0,1:T(8,128)(2,1)S(1)}, u32[]{:S(2)}) copy-start(bf16[960,320]{0,1:T(8,128)(2,1)S(1)} %get-tuple-element.1143) | copy-start | bytes 1843204 | tf_op jit(solution)/shard_map/cond
  855.3 15.3 %copy-start.22 = (bf16[960,320]{0,1:T(8,128)(2,1)}, bf16[960,320]{0,1:T(8,128)(2,1)S(1)}, u32[]{:S(2)}) copy-start(bf16[960,320]{0,1:T(8,128)(2,1)S(1)} %get-tuple-element.564) | copy-start | bytes 1843204 | tf_op jit(solution)/shard_map/cond
  873.5 12.4 slice-start.16
  928.0 10.9 copy-start.77
  928.0 11.9 copy-start.69
  934.2 10.0 copy-start.46
  934.3 10.0 copy-start.75
  934.4 10.8 copy-start.44
  934.4 10.8 copy-start.72
  962.9 12.0 copy-start.31
  962.9 12.0 copy-start.61
  982.0 12.0 copy-start.25
  982.0 12.0 copy-start.59
  982.0 13.0 copy-start.48
  982.0 13.0 copy-start.73
  1013.8 12.4 copy-start.32
  1038.9 20.9 %slice-start.18 = ((s8[9830400]{0:T(1024)(128)(4,1)}), s8[1441792]{0:T(1024)(128)(4,1)S(1)}, s32[]{:S(2)}) async-start(s8[9830400]{0:T(1024)(128)(4,1)} %bitcast.940), calls=%async_computation.24 | async-start | bytes 2883584
  1107.4 374.0 %copy-start.83 = (bf16[1,2,64,960]{3,2,1,0:T(8,128)(2,1)}, bf16[1,2,64,960]{3,2,1,0:T(8,128)(2,1)S(1)}, u32[]{:S(2)}) copy-start(bf16[1,2,64,960]{3,2,1,0:T(8,128)(2,1)S(1)} %get-tuple-element.1332) | copy-start | bytes 737284
  (82 other events, 355.4 us)
Sparse Core Ops, SparseCore 0:
  11.4 71.4 all-gather.5
  86.2 67.3 all-gather.7
  157.0 83.9 all-gather.9
  244.3 85.3 all-gather.11
  332.5 69.7 all-gather.13
  1102.7 364.7 all-reduce.6
where the time goes:
time: 1500 us; the launch traced here: 1490 us
  blocking collectives  545 us (36%)
  waiting for transfers between devices  399 us (27%)
  local copies, waits for them, and re-layouts  291 us (19%)
  matrix products  152 us (10%)
  other arithmetic  75 us (5%)
  between operations  15.9 us (1%)
    unnamed x7, waiting for transfers between devices  361 us
    all_gather x1, blocking collectives, body(): lax.all_gather(w_value, 'dp', axis=1, tiled=True)  188 us
    all_gather x1, blocking collectives, body(): lax.all_gather(w_key, 'dp', axis=1, tiled=True)  184 us
    squeeze x1, blocking collectives, body(): weights = tuple((piece[0] for piece in gathered))  174 us
    unnamed x147, local copies, waits for them, and re-layouts  94.2 us
    reshape x9, local copies, waits for them, and re-layouts, flat_grads(): pieces = [grad.reshape(owner_count, -1) for grad in grads]  52.9 us
    ppermute x4, waiting for transfers between devices, from_behind(): lax.ppermute(value, axis, [(source, source + steps) for source in range(f...  38.7 us
    dynamic_slice x30, local copies, waits for them, and re-layouts, store_slot(): current = lax.dynamic_index_in_dim(buffer, slot_idx, 0, keepdims=False)  31.6 us
  transfers between devices with their start and end apart: 10, of which 3 were waited for; matrix products, arithmetic and copies ran while one was open for 6% of the time, Pallas kernels for 0%

commit v1 on v0

v1 whole, which is shorter than its diff:
```python
import jax
import jax.numpy as jnp
from jax import lax
from jax.sharding import PartitionSpec as P

D = 960
HEADS = 15
KV_HEADS = 5
GROUP = HEADS // KV_HEADS
HEAD_DIM = 64
FF = 2560
QD = 960
KVD = 320
OWNERS = 64
SLOT = 15
PADDED = 16
DOWN_ROWS = 40

norm_eps = 1e-05
masked_score = -1e30
rope_base = 10000.0

f32 = jnp.float32
bf16 = jnp.bfloat16


def gray(value):
    return value ^ (value >> 1)


AXIS_SHIFT = {"y": 4, "z": 2, "x": 0}
BITS = (("y", 1), ("y", 0), ("z", 1), ("z", 0), ("x", 1), ("x", 0))


def partner_pairs(bit):
    axis, place = bit
    shift = AXIS_SHIFT[axis]
    pairs = []
    for source in range(OWNERS):
        coordinate = (source >> shift) & 3
        other = gray(gray(coordinate) ^ (1 << place))
        pairs.append((source, source + ((other - coordinate) << shift)))
    return pairs


def owner_of(position):
    me = lax.axis_index("dp")
    owner = 0
    for shift in (4, 2, 0):
        owner = owner + (gray(gray((me >> shift) & 3) ^ ((position >> shift) & 3)) << shift)
    return owner


def dot(left, right):
    return jnp.dot(left, right, preferred_element_type=f32)


def dot_t(left, right):
    return lax.dot_general(left, right, (((1,), (1,)), ((), ())), preferred_element_type=f32)


def spread_matrix():
    row = lax.broadcasted_iota(jnp.int32, (D, OWNERS * PADDED), 0)
    col = lax.broadcasted_iota(jnp.int32, (D, OWNERS * PADDED), 1)
    return ((row == SLOT * (col // PADDED) + col % PADDED) & (col % PADDED < SLOT)).astype(bf16)


def own_spread():
    row = lax.broadcasted_iota(jnp.int32, (OWNERS * PADDED, D), 0)
    col = lax.broadcasted_iota(jnp.int32, (OWNERS * PADDED, D), 1)
    owner = owner_of(row // PADDED)
    return ((col == SLOT * owner + row % PADDED) & (row % PADDED < SLOT)).astype(bf16)


def gather_rows(values, spread):
    high = values.astype(bf16)
    low = (values - high.astype(f32)).astype(bf16)
    return dot_t(high, spread) + dot_t(low, spread)


def geometry(starts):
    rows = starts.shape[-1]
    local = jnp.arange(rows, dtype=jnp.int32)
    live = starts <= local
    position = jnp.where(live, local - starts, 0).astype(f32)
    frequency = rope_base ** (-2.0 * jnp.arange(HEAD_DIM // 2, dtype=f32) / HEAD_DIM)
    angles = position[..., None, None] * frequency
    causal = local[None, :] <= local[:, None]
    inside = local >= starts[..., None]
    diagonal = local[None, :] == local[:, None]
    allowed = causal & inside | diagonal
    return live.astype(f32).reshape(-1, 1), jnp.cos(angles), jnp.sin(angles), allowed


def rotate(values, cosine, sine):
    half = HEAD_DIM // 2
    first, second = values[..., :half], values[..., half:]
    return jnp.concatenate(
        [first * cosine - second * sine, second * cosine + first * sine], axis=-1
    )


def norm_parts(values):
    inverse = lax.rsqrt(jnp.mean(values * values, axis=-1, keepdims=True) + norm_eps)
    return values * inverse, inverse


def norm_back(grad, normal, inverse, gain):
    scaled = grad * gain
    return inverse * (scaled - normal * jnp.mean(scaled * normal, axis=-1, keepdims=True))


def forward(source, weights, geo, spread):
    w_query, w_key, w_value, w_output, w_gate, w_up, w_down, attn_gain, ffn_gain = weights
    live, cosine, sine, allowed = geo
    micro, rows = cosine.shape[:2]
    h = source.astype(f32)
    n1, r1 = norm_parts(h)
    a = (n1 * attn_gain).astype(bf16)
    a_wide = dot(a, spread).astype(bf16)
    q = rotate(dot(a_wide, w_query).reshape(micro, rows, HEADS, HEAD_DIM), cosine, sine)
    k = rotate(dot(a_wide, w_key).reshape(micro, rows, KV_HEADS, HEAD_DIM), cosine, sine)
    v = dot(a_wide, w_value).astype(bf16).reshape(micro, rows, KV_HEADS, HEAD_DIM)
    q = q.astype(bf16).reshape(micro, rows, KV_HEADS, GROUP, HEAD_DIM)
    k = k.astype(bf16)
    s = jnp.einsum("bqhgd,bkhd->bhgqk", q, k, preferred_element_type=f32) * HEAD_DIM**-0.5
    s = jnp.where(allowed[:, None, None], s, masked_score)
    e = jnp.exp(s - jnp.max(s, axis=-1, keepdims=True))
    p = e / jnp.sum(e, axis=-1, keepdims=True)
    p_low = p.astype(bf16)
    o = jnp.einsum("bhgqk,bkhd->bqhgd", p_low, v, preferred_element_type=f32)
    o = o.reshape(micro * rows, QD).astype(bf16)
    m = h + dot(dot(o, spread).astype(bf16), w_output)
    n2, r2 = norm_parts(m)
    b = (n2 * ffn_gain).astype(bf16)
    b_wide = dot(b, spread).astype(bf16)
    gate = dot(b_wide, w_gate)
    up = dot(b_wide, w_up)
    hidden = (gate * jax.nn.sigmoid(gate) * up).astype(bf16)
    result = ((m + dot(hidden, w_down)) * live).astype(bf16)
    return result, (n1, r1, a, q, k, v, p, p_low, o, n2, r2, b, gate, up, hidden)


def backward(saved, upstream, weights, geo, spread):
    w_query, w_key, w_value, w_output, w_gate, w_up, w_down, attn_gain, ffn_gain = weights
    n1, r1, a, q, k, v, p, p_low, o, n2, r2, b, gate, up, hidden = saved
    live, cosine, sine, allowed = geo
    micro, rows = cosine.shape[:2]
    d3 = upstream.astype(f32) * live
    d3_low = d3.astype(bf16)
    dhidden = dot_t(d3_low, w_down)
    sig = jax.nn.sigmoid(gate)
    dg = (dhidden * up * sig * (1.0 + gate * (1.0 - sig))).astype(bf16)
    du = (dhidden * gate * sig).astype(bf16)
    db = gather_rows(dot_t(dg, w_gate) + dot_t(du, w_up), spread)
    dm = d3 + norm_back(db, n2, r2, ffn_gain)
    dffn = jnp.sum(db * n2, axis=0)
    dm_low = dm.astype(bf16)
    do = dot_t(dot_t(dm_low, w_output).astype(bf16), spread).astype(bf16)
    do = do.reshape(micro, rows, KV_HEADS, GROUP, HEAD_DIM)
    dp = jnp.einsum("bqhgd,bkhd->bhgqk", do, v, preferred_element_type=f32)
    dv = jnp.einsum("bhgqk,bqhgd->bkhd", p_low, do, preferred_element_type=f32)
    ds = (p * (dp - jnp.sum(p * dp, axis=-1, keepdims=True))).astype(bf16)
    dq = jnp.einsum("bhgqk,bkhd->bqhgd", ds, k, preferred_element_type=f32) * HEAD_DIM**-0.5
    dk = jnp.einsum("bhgqk,bqhgd->bkhd", ds, q, preferred_element_type=f32) * HEAD_DIM**-0.5
    dq = rotate(dq.reshape(micro, rows, HEADS, HEAD_DIM), cosine, -sine)
    dq = dq.reshape(micro * rows, QD).astype(bf16)
    dk = rotate(dk, cosine, -sine).reshape(micro * rows, KVD).astype(bf16)
    dv = dv.reshape(micro * rows, KVD).astype(bf16)
    da = gather_rows(dot_t(dq, w_query) + dot_t(dk, w_key) + dot_t(dv, w_value), spread)
    dh = dm + norm_back(da, n1, r1, attn_gain)
    dattn = jnp.sum(da * n1, axis=0)
    return dh.astype(bf16), (d3_low, dg, du, dm_low, dq, dk, dv, dattn, dffn)


def blocks(left_t, rows):
    return left_t.reshape((2,) * 6 + (rows, left_t.shape[-1]))


def pick(array, dim, index):
    return lax.index_in_dim(array, index, dim, keepdims=False)


def product(left_t, right):
    flat = left_t.reshape(-1, left_t.shape[-1])
    return dot(flat, right).reshape(left_t.shape[:-1] + (right.shape[-1],))


def first_halves(left_t, right, order, extra=None):
    dim = BITS.index(order[0])
    halves = []
    for index in (1, 0):
        value = product(pick(left_t, dim, index), right)
        if extra is not None:
            value = value + pick(extra, dim, index)
        halves.append(value.astype(bf16))
    return halves[1], halves[0]


def rotations(place, then):
    axes = "yzx"
    result = []
    for turn in range(3):
        turned = axes[turn:] + axes[:turn]
        result.append(tuple((axis, place) for axis in turned) + tuple((axis, then) for axis in turned))
    return result


ORDERS = (rotations(1, 0), rotations(0, 1))


def halving(kept, sent, order, left, last):
    bit = order[0]
    left = [other for other in left if other != bit]
    arrived = lax.ppermute(sent, "dp", partner_pairs(bit))
    if len(order) == 1:
        return (kept.astype(f32) + arrived.astype(f32)), None, left
    if last:
        return (kept.astype(f32) + arrived.astype(f32)).astype(bf16), None, left
    dim = left.index(order[1])
    next_sent = pick(kept, dim, 1).astype(f32) + pick(arrived, dim, 1).astype(f32)
    next_kept = pick(kept, dim, 0).astype(f32) + pick(arrived, dim, 0).astype(f32)
    return next_kept.astype(bf16), next_sent.astype(bf16), left


def reduce_three(members, orders):
    after = []
    for (left_t, right, extra), order in zip(members, orders):
        kept, sent = first_halves(left_t, right, order, extra)
        left = list(BITS)
        for step in range(3):
            kept, sent, left = halving(kept, sent, order[step:], left, step == 2)
        after.append(kept)
    return after, left


def finish(value, left, order):
    dim = left.index(order[0])
    kept, sent = pick(value, dim, 0), pick(value, dim, 1)
    for step in range(3):
        kept, sent, left = halving(kept, sent, order[step:], left, False)
    return kept


def xor_order(left_t):
    width = left_t.shape[-1]
    value = left_t.reshape(4, 4, 4, DOWN_ROWS, width)
    me = lax.axis_index("dp")
    for dim, shift in enumerate((4, 2, 0)):
        mine = gray((me >> shift) & 3)
        value = jnp.concatenate(
            [lax.dynamic_slice_in_dim(value, gray(mine ^ place), 1, dim) for place in range(4)],
            axis=dim,
        )
    return value


def body(
    inputs,
    starts,
    cotangent,
    w_query,
    w_key,
    w_value,
    w_output,
    w_gate,
    w_up,
    w_down,
    attn_gain,
    ffn_gain,
):
    section = lax.axis_index("section")
    micro, rows = starts.shape
    gains = jnp.concatenate([attn_gain, ffn_gain], axis=1)
    gain_row = jnp.pad(gains, ((0, 0), (0, D - gains.shape[1])))
    blank = jnp.zeros((1, D), bf16)
    slabs = (
        w_query[0],
        w_output[0],
        w_gate[0, :, :960],
        w_gate[0, :, 960:1920],
        w_up[0, :, :960],
        w_up[0, :, 960:1920],
        jnp.concatenate([w_gate[0, :, 1920:], w_key[0]], axis=1),
        jnp.concatenate([w_up[0, :, 1920:], w_value[0]], axis=1),
    )
    pieces = []
    for index, slab in enumerate(slabs):
        pieces += [slab, gain_row if index == 0 else blank]
    packed = jnp.concatenate(pieces + [w_down[0]], axis=0)[None]
    everything = lax.all_gather(packed, "dp", axis=0, tiled=True)

    def slab_of(index):
        part = everything[:, PADDED * index : PADDED * (index + 1)]
        return part.reshape(OWNERS * PADDED, D)

    mixed_gate, mixed_up = slab_of(6), slab_of(7)
    all_gains = everything[:, SLOT, : 2 * SLOT].astype(f32)
    weights = (
        slab_of(0),
        mixed_gate[:, 640:],
        mixed_up[:, 640:],
        slab_of(1),
        jnp.concatenate([slab_of(2), slab_of(3), mixed_gate[:, :640]], axis=1),
        jnp.concatenate([slab_of(4), slab_of(5), mixed_up[:, :640]], axis=1),
        everything[:, 8 * PADDED :].reshape(FF, D),
        all_gains[:, :SLOT].reshape(D),
        all_gains[:, SLOT:].reshape(D),
    )
    spread = spread_matrix()
    mine = own_spread()
    geo = geometry(starts)
    first_in = inputs.reshape(micro * rows, D)
    top = cotangent.reshape(micro * rows, D)

    made, _ = forward(first_in, weights, geo, spread)
    arrived = lax.ppermute(made, "section", [(0, 1)])
    source = jnp.where(section == 0, first_in, arrived)
    result, saved = forward(source, weights, geo, spread)
    back, _ = backward(saved, top, weights, geo, spread)
    returned = lax.ppermute(back, "section", [(1, 0)])
    upstream = jnp.where(section == 1, top, returned)
    grad_rows, grads = backward(saved, upstream, weights, geo, spread)
    d3_low, dg, du, dm_low, dq, dk, dv, dattn, dffn = grads
    a, o, b, hidden = saved[2], saved[8], saved[11], saved[14]

    a_t = blocks(dot_t(mine, a).astype(bf16), PADDED)
    o_t = blocks(dot_t(mine, o).astype(bf16), PADDED)
    b_t = blocks(dot_t(mine, b).astype(bf16), PADDED)
    hidden_t = blocks(xor_order(hidden.T), DOWN_ROWS)

    half = FF // 2
    outs = []
    for group, orders in enumerate(ORDERS):
        cut = slice(group * half, (group + 1) * half)
        down_cut = slice(0, 512) if group == 0 else slice(512, D)
        members = (
            (b_t, dg[:, cut], None),
            (b_t, du[:, cut], None),
            (hidden_t, d3_low[:, down_cut], None),
        )
        (gate_part, up_part, down_part), left = reduce_three(members, orders)
        pair = jnp.concatenate([gate_part, up_part], axis=-1)
        outs.append((finish(pair, left, orders[0][3:]), finish(down_part, left, orders[1][3:])))
    grad_gate = jnp.concatenate([outs[0][0][:SLOT, :half], outs[1][0][:SLOT, :half]], axis=1)
    grad_up = jnp.concatenate([outs[0][0][:SLOT, half:], outs[1][0][:SLOT, half:]], axis=1)
    grad_down = jnp.concatenate([outs[0][1], outs[1][1]], axis=1)

    owner = owner_of(jnp.arange(OWNERS, dtype=jnp.int32))
    choose = (owner[:, None] == jnp.arange(OWNERS, dtype=jnp.int32)[None, :]).astype(f32)
    both = jnp.concatenate([dattn.reshape(OWNERS, SLOT), dffn.reshape(OWNERS, SLOT)], axis=1)
    both = jnp.dot(choose, both, precision=lax.Precision.HIGHEST)
    extra = jnp.pad(both[:, None, :], ((0, 0), (SLOT, 0), (0, 512 - 2 * SLOT)))
    extra = extra.reshape((2,) * 6 + extra.shape[1:])
    dqkv = jnp.concatenate([dq, dk, dv], axis=1)
    cuts = (((0, 512), (512, 896), (0, 512)), ((896, 1280), (1280, 1600), (512, 960)))
    ends = []
    for group, orders in enumerate(ORDERS):
        (lo0, hi0), (lo1, hi1), (lo2, hi2) = cuts[group]
        members = (
            (a_t, dqkv[:, lo0:hi0], extra if group == 0 else None),
            (a_t, dqkv[:, lo1:hi1], None),
            (o_t, dm_low[:, lo2:hi2], None),
        )
        parts, left = reduce_three(members, orders)
        ends.append(finish(jnp.concatenate(parts, axis=-1), left, orders[2][3:]))
    dqkv_sum = jnp.concatenate([ends[0][:, :896], ends[1][:, :704]], axis=1)
    grad_output = jnp.concatenate([ends[0][:SLOT, 896:], ends[1][:SLOT, 704:]], axis=1)
    gain_sum = dqkv_sum[SLOT]
    return (
        result.reshape(1, micro, rows, D),
        grad_rows.reshape(1, micro, rows, D),
        dqkv_sum[None, :SLOT, :QD],
        dqkv_sum[None, :SLOT, QD : QD + KVD],
        dqkv_sum[None, :SLOT, QD + KVD :],
        grad_output[None],
        grad_gate[None],
        grad_up[None],
        grad_down[None],
        gain_sum[None, :SLOT],
        gain_sum[None, SLOT : 2 * SLOT],
    )


def solution(mesh):
    split = P("section", "dp", None)
    return jax.shard_map(
        body,
        mesh=mesh,
        in_specs=(P(None, "dp", None), P(None, "dp"), P(None, "dp", None))
        + (split,) * 7
        + (P("section", "dp"),) * 2,
        out_specs=(P("section", None, "dp", None),) * 2
        + (split,) * 7
        + (P("section", "dp"),) * 2,
        check_vma=False,
    )
```

time: 1500 us -> 709 us (0.47)
  blocking collectives: 545 us -> 0 us
  local copies, waits for them, and re-layouts: 291 us -> 152 us
  waiting for transfers between devices: 399 us -> 268 us
  starting transfers between devices: 7.76 us -> 66.3 us
  other arithmetic: 75 us -> 45.4 us
    all_gather x2 -> x0, blocking collectives: 372 us -> none  [the longest x1 188 us: body(): lax.all_gather(w_value, 'dp', axis=1, tiled=True)]
    unnamed x7 -> x1, waiting for transfers between devices: 361 us -> 0.02 us
    squeeze x1 -> x0, blocking collectives: 174 us -> none  [body(): weights = tuple((piece[0] for piece in gathered))]
    ppermute x4 -> x56, waiting for transfers between devices: 38.7 us -> 156 us  [the longest x54 156 us: halving(): arrived = lax.ppermute(sent, 'dp', partner_pairs(bit))]
    all_gather x5 -> x1, waiting for transfers between devices: 0.03 us -> 112 us  [body(): everything = lax.all_gather(packed, 'dp', axis=0, tiled=True)]
    unnamed x147 -> x254, local copies, waits for them, and re-layouts: 94.2 us -> 12.9 us
    ppermute x4 -> x56, starting transfers between devices: 7.51 us -> 66.2 us  [the longest x54 62.5 us: halving(): arrived = lax.ppermute(sent, 'dp', partner_pairs(bit))]
    reshape x16 -> x11, local copies, waits for them, and re-layouts: 60.3 us -> 12.2 us  [the longest x2 3.12 us: backward(): do = do.reshape(micro, rows, KV_HEADS, GROUP, HEAD_DIM)]
  transfers between devices with their start and end apart: 10 -> 57, of which waited for: 3 -> 30; matrix products, arithmetic and copies ran while one was open for 6% -> 12% of each run, Pallas kernels for 0% -> 0%
where the time goes in v1:
time: 709 us; the launch traced here: 696 us
  waiting for transfers between devices  268 us (38%)
  local copies, waits for them, and re-layouts  152 us (21%)
  matrix products  147 us (21%)
  starting transfers between devices  66.3 us (9%)
  other arithmetic  45.4 us (6%)
  between operations  17 us (2%)
    ppermute x54, waiting for transfers between devices, halving(): arrived = lax.ppermute(sent, 'dp', partner_pairs(bit))  156 us
    all_gather x1, waiting for transfers between devices, body(): everything = lax.all_gather(packed, 'dp', axis=0, tiled=True)  112 us
    dot_general x41, matrix products, dot(): return jnp.dot(left, right, preferred_element_type=f32)  78.1 us
    ppermute x54, starting transfers between devices, halving(): arrived = lax.ppermute(sent, 'dp', partner_pairs(bit))  62.5 us
    dot_general x25, matrix products, dot_t(): lax.dot_general(left, right, (((1,), (1,)), ((), ())), preferred_element_...  47.5 us
    concatenate x1, local copies, waits for them, and re-layouts, body(): packed = jnp.concatenate(pieces + [w_down[0]], axis=0)[None]  18.6 us
    convert_element_type x39, other arithmetic, halving(): return (next_kept.astype(bf16), next_sent.astype(bf16), left)  17.7 us
  transfers between devices with their start and end apart: 57, of which 30 were waited for; matrix products, arithmetic and copies ran while one was open for 12% of the time, Pallas kernels for 0%

profile of v1, /device:TPU:0, one launch (start us, length us, event | category | flops | bytes accessed | tf_op | source)
XLA Modules:
  0.0 695.9 jit_solution(18312639597677706957)
XLA Ops:
  11.1 18.6 %concatenate.104 = bf16[168,960]{1,0:T(8,128)(2,1)} concatenate(bf16[15,960]{1,0:T(8,128)(2,1)} %bitcast.888, bf16[1,960]{1,0:T(2,128)(2,1)S(1)} %fusion.272, bf16[15,960]{1,0:T(8,128)(2,1)} %bitcast.889, bf16[1,960]{1,0:T(2,128)(2,1)S(1)} %broadcast.365, bf16[15,960]{1,0:T(8,128)(2,1)S(1)} %get-tuple-element.178, bf16[1,960]{1,0:T(2,128)(2,1)S(1)} %broadcast.365, ...), dimensions={0} | concatenate | bytes 645120 | tf_op jit(solution)/shard_map/concatenate | solution.py:290
  40.9 112.3 %all-gather.3.cloned.1.call-done = bf16[10752,960]{1,0:T(8,128)(2,1)} async-done(((bf16[168,960]{1,0:T(8,128)(2,1)}), bf16[10752,960]{1,0:T(8,128)(2,1)}) %all-gather.3.cloned.1.call-update) | async-done | bytes 20643856 | tf_op jit(solution)/shard_map/all_gather | solution.py:291
  154.1 5.5 slice.1024
  159.6 11.7 %fusion.328 = (bf16[64,16,960]{2,1,0:T(8,128)(2,1)}, bf16[64,16,960]{2,1,0:T(8,128)(2,1)}, bf16[64,16,960]{2,1,0:T(8,128)(2,1)}, bf16[64,16,960]{2,1,0:T(8,128)(...) fusion(bf16[64,168,960]{2,1,0:T(8,128)(2,1)} %bitcast.821), kind=kLoop, calls=%fused_computation.648 | loop fusion | bytes 31457280 | tf_op jit(solution)/shard_map/slice | solution.py:294
  204.2 3.0 fusion.37
  211.4 4.6 multiply_reduce_fusion.7
  217.2 9.6 %concatenate.109 = bf16[1024,2560]{1,0:T(8,128)(2,1)} concatenate(bf16[1024,960]{1,0:T(8,128)(2,1)} %bitcast.847, bf16[1024,960]{1,0:T(8,128)(2,1)} %bitcast.846, bf16[1024,640]{1,0:T(8,128)(2,1)} %slice.1020), dimensions={1} | concatenate | bytes 10485760 | tf_op jit(solution)/shard_map/concatenate | solution.py:304
  231.4 9.6 %concatenate.110 = bf16[1024,2560]{1,0:T(8,128)(2,1)} concatenate(bf16[1024,960]{1,0:T(8,128)(2,1)} %bitcast.845, bf16[1024,960]{1,0:T(8,128)(2,1)} %bitcast.844, bf16[1024,640]{1,0:T(8,128)(2,1)S(1)} %slice.1023), dimensions={1} | concatenate | bytes 10485760 | tf_op jit(solution)/shard_map/concatenate | solution.py:305
  241.0 7.0 %fusion.42 = bf16[128,960]{0,1:T(8,128)(2,1)S(1)} fusion(f32[128,960]{0,1:T(8,128)} %get-tuple-element.159, bf16[2560,960]{1,0:T(8,128)(2,1)} %bitcast.822, bf16[128,1024]{1,0:T(8,128)(2,1)} %copy-done.67, bf16[1024,2560]{1,0:T(8,128)(2,1)} %concatenate.110, f32[128,2560]{1,0:T(8,128)} %fusion.346, f32[128]{0:T(128)S(1)} %mul.607), kind=kOutput, calls=%fused_computation.134 | convolution fusion | flops 1302568960 | bytes 12468736 | tf_op jit(solution)/shard_map/dot_general | solution.py:55
  249.9 5.4 fusion.349
  281.1 4.1 convolution_convert_fusion.25
  285.2 3.3 multiply_reduce_fusion.6
  298.5 2.7 fusion.41
  307.5 4.1 convolution_convert_fusion.36
  353.7 3.7 convolution_convert_fusion.35
  374.3 2.6 fusion.352
  379.6 2.7 convolution_convert_fusion.10
  398.7 2.8 collective-permute-start.5
  431.8 4.3 pad_slice_fusion.1
  436.1 3.7 copy.174
  439.8 3.1 copy.176
  457.9 24.5 %collective-permute-done.18 = bf16[2,2,2,2,16,320]{5,4,2,3,0,1:T(8,128)(2,1)S(1)} collective-permute-done((bf16[2,2,2,2,16,320]{5,4,2,3,0,1:T(8,128)(2,1)S(1)}, bf16[2,2,2,2,16,320]{5,4,2,3,0,1:T(8,128)(2,1)S(1)}, u32[]{:S(2)}, u32[]{:S(2)}) %collective-permute-start.18) | collective-permute-done | bytes 163872 | tf_op jit(solution)/shard_map/ppermute | solution.py:215
  488.4 3.9 collective-permute-done.19
  494.7 3.2 collective-permute-done.15
  501.7 19.8 %collective-permute-done.7 = bf16[2,2,2,16,384]{4,3,2,1,0:T(8,128)(2,1)S(1)} collective-permute-done((bf16[2,2,2,16,384]{4,3,2,1,0:T(8,128)(2,1)S(1)}, bf16[2,2,2,16,384]{4,3,2,1,0:T(8,128)(2,1)S(1)}, u32[]{:S(2)}, u32[]{:S(2)}) %collective-permute-start.7) | collective-permute-done | bytes 98336 | tf_op jit(solution)/shard_map/ppermute | solution.py:215
  523.1 3.0 collective-permute-done.16
  529.2 4.4 collective-permute-done.3
  534.7 3.9 collective-permute-done.22
  541.7 3.6 collective-permute-done.10
  548.3 3.5 collective-permute-done.4
  554.9 3.2 collective-permute-done.23
  559.7 4.1 collective-permute-done.24
  565.8 3.3 collective-permute-done.25
  569.1 5.5 collective-permute-done.11
  576.2 4.1 collective-permute-done.12
  584.1 2.8 collective-permute-done.13
  596.1 13.1 %collective-permute-done.29 = bf16[2,2,2,2,2,16,1280]{6,5,4,2,1,3,0:T(8,128)(2,1)S(1)} collective-permute-done((bf16[2,2,2,2,2,16,1280]{6,5,4,2,1,3,0:T(8,128)(2,1)S(1)}, bf16[2,2,2,2,2,16,1280]{6,5,4,2,1,3,0:T(8,128)(2,1)S(1)}, u32[]{:S(2)}, u32[]{:S(2)}) %collective-permute-start.29) | collective-permute-done | bytes 1310752 | tf_op jit(solution)/shard_map/ppermute | solution.py:215
  609.6 4.2 collective-permute-done.38
  618.7 2.6 collective-permute-start.46
  621.4 3.8 collective-permute-done.52
  628.9 5.2 collective-permute-done.53
  636.9 4.4 collective-permute-done.54
  644.7 8.8 %collective-permute-done.55 = bf16[40,448]{1,0:T(8,128)(2,1)S(1)} collective-permute-done((bf16[40,448]{1,0:T(8,128)(2,1)S(1)}, bf16[40,448]{1,0:T(8,128)(2,1)S(1)}, u32[]{:S(2)}, u32[]{:S(2)}) %collective-permute-start.55) | collective-permute-done | bytes 35872 | tf_op jit(solution)/shard_map/ppermute | solution.py:215
  656.3 2.8 collective-permute-done.47
  660.7 3.2 collective-permute-done.48
  669.2 5.2 collective-permute-done.41
  675.5 5.6 collective-permute-done.42
  682.5 4.4 collective-permute-done.43
  (609 shorter events, 298.5 us)
Async XLA Ops:
  7.2 146.0 %all-gather.3.cloned.1.call-start = ((), (), s32[]{:S(2)}) async-start(), calls=%async_computation | async-start | bytes 22364160 | tf_op jit(solution)/shard_map/all_gather | solution.py:291
  248.1 7.3 %collective-permute-start = (bf16[128,960]{0,1:T(8,128)(2,1)S(1)}, bf16[128,960]{0,1:T(8,128)(2,1)S(1)}, u32[]{:S(2)}, u32[]{:S(2)}) collective-permute-start(bf16[128,960]{0,1:T(8,128)(2,1)S(1)} %fusion.42), channel_id=1, source_target_pairs={{0,64},{1,65},{2,66},{3,67},{4,68},{5,69},{6,70},{7,71},{8,72},{9,... | collective-permute-start | bytes 737288 | tf_op jit(solution)/shard_map/ppermute | solution.py:317
  398.7 54.5 %collective-permute-start.5 = (bf16[2,2,2,2,2,16,384]{6,5,4,2,1,3,0:T(8,128)(2,1)}, bf16[2,2,2,2,2,16,384]{6,5,4,2,1,3,0:T(8,128)(2,1)}, u32[]{:S(2)}, u32[]{:S(2)}) collective-permute-start(bf16[2,2,2,2,2,16,384]{6,5,4,2,1,3,0:T(8,128)(2,1)} %convolution_convert_fusion.22), channel_id=1, source_target_pairs={{0,12},{1,13},{2,14},{3,15},{4,8},{5,9},{6,10},{7,11},{8,4},{9,5},... | collective-permute-start | bytes 1179656 | tf_op jit(solution)/shard_map/ppermute | solution.py:215
  401.5 48.7 %collective-permute-start.14 = (bf16[2,2,2,2,2,16,384]{6,5,1,3,0,4,2:T(8,128)(2,1)}, bf16[2,2,2,2,2,16,384]{6,5,1,3,0,4,2:T(8,128)(2,1)}, u32[]{:S(2)}, u32[]{:S(2)}) collective-permute-start(bf16[2,2,2,2,2,16,384]{6,5,1,3,0,4,2:T(8,128)(2,1)} %convolution_convert_fusion.20), channel_id=1, source_target_pairs={{0,16},{1,17},{2,18},{3,19},{4,20},{5,21},{6,22},{7,23},{8,24},{9,... | collective-permute-start | bytes 1179656 | tf_op jit(solution)/shard_map/ppermute | solution.py:215
  404.0 43.2 %collective-permute-start.17 = (bf16[2,2,2,2,2,16,320]{6,5,2,3,0,1,4:T(8,128)(2,1)}, bf16[2,2,2,2,2,16,320]{6,5,2,3,0,1,4:T(8,128)(2,1)}, u32[]{:S(2)}, u32[]{:S(2)}) collective-permute-start(bf16[2,2,2,2,2,16,320]{6,5,2,3,0,1,4:T(8,128)(2,1)} %convolution_convert_fusion.18), channel_id=1, source_target_pairs={{0,4},{1,5},{2,6},{3,7},{4,0},{5,1},{6,2},{7,3},{8,12},{9,13},{10,... | collective-permute-start | bytes 983048 | tf_op jit(solution)/shard_map/ppermute | solution.py:215
  411.2 73.0 %collective-permute-start.8 = (bf16[2,2,2,2,2,16,512]{6,5,4,3,1,2,0:T(8,128)(2,1)}, bf16[2,2,2,2,2,16,512]{6,5,4,3,1,2,0:T(8,128)(2,1)}, u32[]{:S(2)}, u32[]{:S(2)}) collective-permute-start(bf16[2,2,2,2,2,16,512]{6,5,4,3,1,2,0:T(8,128)(2,1)} %convolution_convert_fusion.14), channel_id=1, source_target_pairs={{0,3},{1,2},{2,1},{3,0},{4,7},{5,6},{6,5},{7,4},{8,11},{9,10},{10,... | collective-permute-start | bytes 1572872 | tf_op jit(solution)/shard_map/ppermute | solution.py:215
  412.7 43.9 %collective-permute-start.20 = (bf16[2,2,2,2,2,16,448]{6,5,2,4,0,3,1:T(8,128)(2,1)}, bf16[2,2,2,2,2,16,448]{6,5,2,4,0,3,1:T(8,128)(2,1)}, u32[]{:S(2)}, u32[]{:S(2)}) collective-permute-start(bf16[2,2,2,2,2,16,448]{6,5,2,4,0,3,1:T(8,128)(2,1)} %convolution_convert_fusion.12), channel_id=1, source_target_pairs={{0,1},{1,0},{2,3},{3,2},{4,5},{5,4},{6,7},{7,6},{8,9},{9,8},{10,11... | collective-permute-start | bytes 1376264 | tf_op jit(solution)/shard_map/ppermute | solution.py:215
  447.3 134.9 %collective-permute-start.50 = (bf16[2,2,2,2,2,40,448]{6,5,4,0,2,3,1:T(8,128)(2,1)}, bf16[2,2,2,2,2,40,448]{6,5,4,0,2,3,1:T(8,128)(2,1)}, u32[]{:S(2)}, u32[]{:S(2)}) collective-permute-start(bf16[2,2,2,2,2,40,448]{6,5,4,0,2,3,1:T(8,128)(2,1)} %convolution_convert_fusion.8), channel_id=1, source_target_pairs={{0,1},{1,0},{2,3},{3,2},{4,5},{5,4},{6,7},{7,6},{8,9},{9,8},{10,11... | collective-permute-start | bytes 3440648 | tf_op jit(solution)/shard_map/ppermute | solution.py:215
  450.3 138.6 %collective-permute-start.44 = (bf16[2,2,2,2,2,40,512]{6,5,4,3,1,2,0:T(8,128)(2,1)}, bf16[2,2,2,2,2,40,512]{6,5,4,3,1,2,0:T(8,128)(2,1)}, u32[]{:S(2)}, u32[]{:S(2)}) collective-permute-start(bf16[2,2,2,2,2,40,512]{6,5,4,3,1,2,0:T(8,128)(2,1)} %convolution_convert_fusion.10), channel_id=1, source_target_pairs={{0,3},{1,2},{2,1},{3,0},{4,7},{5,6},{6,5},{7,4},{8,11},{9,10},{10,... | collective-permute-start | bytes 3932168 | tf_op jit(solution)/shard_map/ppermute | solution.py:215
  453.2 34.3 %collective-permute-start.2 = (bf16[2,2,2,2,2,16,512]{6,5,4,2,0,3,1:T(8,128)(2,1)S(1)}, bf16[2,2,2,2,2,16,512]{6,5,4,2,0,3,1:T(8,128)(2,1)S(1)}, u32[]{:S(2)}, u32[]{:S(2)}) collective-permute-start(bf16[2,2,2,2,2,16,512]{6,5,4,2,0,3,1:T(8,128)(2,1)S(1)} %fusion.34), channel_id=1, source_target_pairs={{0,48},{1,49},{2,50},{3,51},{4,52},{5,53},{6,54},{7,55},{8,56},{9,... | collective-permute-start | bytes 1572872 | tf_op jit(solution)/shard_map/ppermute | solution.py:215
  456.5 25.9 %collective-permute-start.18 = (bf16[2,2,2,2,16,320]{5,4,2,3,0,1:T(8,128)(2,1)S(1)}, bf16[2,2,2,2,16,320]{5,4,2,3,0,1:T(8,128)(2,1)S(1)}, u32[]{:S(2)}, u32[]{:S(2)}) collective-permute-start(bf16[2,2,2,2,16,320]{5,4,2,3,0,1:T(8,128)(2,1)S(1)} %get-tuple-element.78), channel_id=1, source_target_pairs={{0,1},{1,0},{2,3},{3,2},{4,5},{5,4},{6,7},{7,6},{8,9},{9,8},{10,11... | collective-permute-start | bytes 491528 | tf_op jit(solution)/shard_map/ppermute | solution.py:215
  482.4 107.9 %collective-permute-start.26 = (bf16[2,2,2,2,2,16,1280]{6,5,4,2,0,3,1:T(8,128)(2,1)}, bf16[2,2,2,2,2,16,1280]{6,5,4,2,0,3,1:T(8,128)(2,1)}, u32[]{:S(2)}, u32[]{:S(2)}) collective-permute-start(bf16[2,2,2,2,2,16,1280]{6,5,4,2,0,3,1:T(8,128)(2,1)} %convolution_convert_fusion.6), channel_id=1, source_target_pairs={{0,48},{1,49},{2,50},{3,51},{4,52},{5,53},{6,54},{7,55},{8,56},{9,... | collective-permute-start | bytes 3932168 | tf_op jit(solution)/shard_map/ppermute | solution.py:215
  484.2 9.9 %collective-permute-start.6 = (bf16[2,2,2,2,16,384]{5,4,3,2,1,0:T(8,128)(2,1)S(1)}, bf16[2,2,2,2,16,384]{5,4,3,2,1,0:T(8,128)(2,1)S(1)}, u32[]{:S(2)}, u32[]{:S(2)}) collective-permute-start(bf16[2,2,2,2,16,384]{5,4,3,2,1,0:T(8,128)(2,1)S(1)} %get-tuple-element.76), channel_id=1, source_target_pairs={{0,3},{1,2},{2,1},{3,0},{4,7},{5,6},{6,5},{7,4},{8,11},{9,10},{10,... | collective-permute-start | bytes 589832 | tf_op jit(solution)/shard_map/ppermute | solution.py:215
  492.3 5.7 collective-permute-start.15
  494.0 6.5 collective-permute-start.21
  497.9 30.6 %collective-permute-start.9 = (bf16[2,2,2,2,16,512]{5,4,3,2,0,1:T(8,128)(2,1)S(1)}, bf16[2,2,2,2,16,512]{5,4,3,2,0,1:T(8,128)(2,1)S(1)}, u32[]{:S(2)}, u32[]{:S(2)}) collective-permute-start(bf16[2,2,2,2,16,512]{5,4,3,2,0,1:T(8,128)(2,1)S(1)} %get-tuple-element.60), channel_id=1, source_target_pairs={{0,48},{1,49},{2,50},{3,51},{4,52},{5,53},{6,54},{7,55},{8,56},{9,... | collective-permute-start | bytes 786440 | tf_op jit(solution)/shard_map/ppermute | solution.py:215
  500.5 20.9 %collective-permute-start.7 = (bf16[2,2,2,16,384]{4,3,2,1,0:T(8,128)(2,1)S(1)}, bf16[2,2,2,16,384]{4,3,2,1,0:T(8,128)(2,1)S(1)}, u32[]{:S(2)}, u32[]{:S(2)}) collective-permute-start(bf16[2,2,2,16,384]{4,3,2,1,0:T(8,128)(2,1)S(1)} %fusion.229), channel_id=1, source_target_pairs={{0,48},{1,49},{2,50},{3,51},{4,52},{5,53},{6,54},{7,55},{8,56},{9,... | collective-permute-start | bytes 294920 | tf_op jit(solution)/shard_map/ppermute | solution.py:215
  526.1 7.6 %collective-permute-start.3 = (bf16[2,2,2,2,16,512]{5,4,3,2,1,0:T(8,128)(2,1)S(1)}, bf16[2,2,2,2,16,512]{5,4,3,2,1,0:T(8,128)(2,1)S(1)}, u32[]{:S(2)}, u32[]{:S(2)}) collective-permute-start(bf16[2,2,2,2,16,512]{5,4,3,2,1,0:T(8,128)(2,1)S(1)} %fusion.147), channel_id=1, source_target_pairs={{0,12},{1,13},{2,14},{3,15},{4,8},{5,9},{6,10},{7,11},{8,4},{9,5},... | collective-permute-start | bytes 786440 | tf_op jit(solution)/shard_map/ppermute | solution.py:215
  528.5 65.3 %collective-permute-start.35 = (bf16[2,2,2,2,2,16,1280]{6,5,3,1,0,4,2:T(8,128)(2,1)}, bf16[2,2,2,2,2,16,1280]{6,5,3,1,0,4,2:T(8,128)(2,1)}, u32[]{:S(2)}, u32[]{:S(2)}) collective-permute-start(bf16[2,2,2,2,2,16,1280]{6,5,3,1,0,4,2:T(8,128)(2,1)} %convolution_convert_fusion.2), channel_id=1, source_target_pairs={{0,16},{1,17},{2,18},{3,19},{4,20},{5,21},{6,22},{7,23},{8,24},{9,... | collective-permute-start | bytes 3932168 | tf_op jit(solution)/shard_map/ppermute | solution.py:215
  538.6 6.7 collective-permute-start.10
  545.3 6.5 collective-permute-start.4
  551.8 6.4 collective-permute-start.23
  558.2 5.6 collective-permute-start.24
  569.1 5.5 collective-permute-start.11
  574.7 5.6 collective-permute-start.12
  580.3 28.9 %collective-permute-start.29 = (bf16[2,2,2,2,2,16,1280]{6,5,4,2,1,3,0:T(8,128)(2,1)S(1)}, bf16[2,2,2,2,2,16,1280]{6,5,4,2,1,3,0:T(8,128)(2,1)S(1)}, u32[]{:S(2)}, u32[]{:S(2)}) collective-permute-start(bf16[2,2,2,2,2,16,1280]{6,5,4,2,1,3,0:T(8,128)(2,1)S(1)} %copy-done.36), channel_id=1, source_target_pairs={{0,12},{1,13},{2,14},{3,15},{4,8},{5,9},{6,10},{7,11},{8,4},{9,5},... | collective-permute-start | bytes 3932168 | tf_op jit(solution)/shard_map/ppermute | solution.py:215
  586.9 26.9 %collective-permute-start.38 = (bf16[2,2,2,2,2,16,1280]{6,5,3,2,0,1,4:T(8,128)(2,1)S(1)}, bf16[2,2,2,2,2,16,1280]{6,5,3,2,0,1,4:T(8,128)(2,1)S(1)}, u32[]{:S(2)}, u32[]{:S(2)}) collective-permute-start(bf16[2,2,2,2,2,16,1280]{6,5,3,2,0,1,4:T(8,128)(2,1)S(1)} %copy-done.35), channel_id=1, source_target_pairs={{0,4},{1,5},{2,6},{3,7},{4,0},{5,1},{6,2},{7,3},{8,12},{9,13},{10,... | collective-permute-start | bytes 3932168 | tf_op jit(solution)/shard_map/ppermute | solution.py:215
  588.9 29.0 %collective-permute-start.51 = (bf16[2,2,2,2,40,448]{5,4,3,0,1,2:T(8,128)(2,1)S(1)}, bf16[2,2,2,2,40,448]{5,4,3,0,1,2:T(8,128)(2,1)S(1)}, u32[]{:S(2)}, u32[]{:S(2)}) collective-permute-start(bf16[2,2,2,2,40,448]{5,4,3,0,1,2:T(8,128)(2,1)S(1)} %get-tuple-element.50), channel_id=1, source_target_pairs={{0,16},{1,17},{2,18},{3,19},{4,20},{5,21},{6,22},{7,23},{8,24},{9,... | collective-permute-start | bytes 1720328 | tf_op jit(solution)/shard_map/ppermute | solution.py:215
  590.3 27.8 %collective-permute-start.45 = (bf16[2,2,2,2,40,512]{5,4,3,2,1,0:T(8,128)(2,1)S(1)}, bf16[2,2,2,2,40,512]{5,4,3,2,1,0:T(8,128)(2,1)S(1)}, u32[]{:S(2)}, u32[]{:S(2)}) collective-permute-start(bf16[2,2,2,2,40,512]{5,4,3,2,1,0:T(8,128)(2,1)S(1)} %fusion.68), channel_id=1, source_target_pairs={{0,48},{1,49},{2,50},{3,51},{4,52},{5,53},{6,54},{7,55},{8,56},{9,... | collective-permute-start | bytes 1966088 | tf_op jit(solution)/shard_map/ppermute | solution.py:215
  593.8 24.9 %collective-permute-start.27 = (bf16[2,2,2,2,16,1280]{5,4,3,2,1,0:T(8,128)(2,1)S(1)}, bf16[2,2,2,2,16,1280]{5,4,3,2,1,0:T(8,128)(2,1)S(1)}, u32[]{:S(2)}, u32[]{:S(2)}) collective-permute-start(bf16[2,2,2,2,16,1280]{5,4,3,2,1,0:T(8,128)(2,1)S(1)} %fusion.67), channel_id=1, source_target_pairs={{0,12},{1,13},{2,14},{3,15},{4,8},{5,9},{6,10},{7,11},{8,4},{9,5},... | collective-permute-start | bytes 1966088 | tf_op jit(solution)/shard_map/ppermute | solution.py:215
  609.2 18.2 %collective-permute-start.36 = (bf16[2,2,2,2,16,1280]{5,4,2,1,0,3:T(8,128)(2,1)S(1)}, bf16[2,2,2,2,16,1280]{5,4,2,1,0,3:T(8,128)(2,1)S(1)}, u32[]{:S(2)}, u32[]{:S(2)}) collective-permute-start(bf16[2,2,2,2,16,1280]{5,4,2,1,0,3:T(8,128)(2,1)S(1)} %get-tuple-element.56), channel_id=1, source_target_pairs={{0,4},{1,5},{2,6},{3,7},{4,0},{5,1},{6,2},{7,3},{8,12},{9,13},{10,... | collective-permute-start | bytes 1966088 | tf_op jit(solution)/shard_map/ppermute | solution.py:215
  613.8 21.7 %collective-permute-start.30 = (bf16[2,2,2,2,16,1280]{5,4,3,2,1,0:T(8,128)(2,1)S(1)}, bf16[2,2,2,2,16,1280]{5,4,3,2,1,0:T(8,128)(2,1)S(1)}, u32[]{:S(2)}, u32[]{:S(2)}) collective-permute-start(bf16[2,2,2,2,16,1280]{5,4,3,2,1,0:T(8,128)(2,1)S(1)} %get-tuple-element.52), channel_id=1, source_target_pairs={{0,3},{1,2},{2,1},{3,0},{4,7},{5,6},{6,5},{7,4},{8,11},{9,10},{10,... | collective-permute-start | bytes 1966088 | tf_op jit(solution)/shard_map/ppermute | solution.py:215
  617.9 25.8 %collective-permute-start.39 = (bf16[2,2,2,2,16,1280]{5,4,3,2,0,1:T(8,128)(2,1)S(1)}, bf16[2,2,2,2,16,1280]{5,4,3,2,0,1:T(8,128)(2,1)S(1)}, u32[]{:S(2)}, u32[]{:S(2)}) collective-permute-start(bf16[2,2,2,2,16,1280]{5,4,3,2,0,1:T(8,128)(2,1)S(1)} %get-tuple-element.54), channel_id=1, source_target_pairs={{0,1},{1,0},{2,3},{3,2},{4,5},{5,4},{6,7},{7,6},{8,9},{9,8},{10,11... | collective-permute-start | bytes 1966088 | tf_op jit(solution)/shard_map/ppermute | solution.py:215
  618.1 7.2 %collective-permute-start.52 = (bf16[2,2,2,40,448]{4,3,2,0,1:T(8,128)(2,1)S(1)}, bf16[2,2,2,40,448]{4,3,2,0,1:T(8,128)(2,1)S(1)}, u32[]{:S(2)}, u32[]{:S(2)}) collective-permute-start(bf16[2,2,2,40,448]{4,3,2,0,1:T(8,128)(2,1)S(1)} %fusion.122), channel_id=1, source_target_pairs={{0,4},{1,5},{2,6},{3,7},{4,0},{5,1},{6,2},{7,3},{8,12},{9,13},{10,... | collective-permute-start | bytes 860168 | tf_op jit(solution)/shard_map/ppermute | solution.py:215
  618.7 34.8 %collective-permute-start.46 = (bf16[2,2,2,40,512]{4,3,2,1,0:T(8,128)(2,1)S(1)}, bf16[2,2,2,40,512]{4,3,2,1,0:T(8,128)(2,1)S(1)}, u32[]{:S(2)}, u32[]{:S(2)}) collective-permute-start(bf16[2,2,2,40,512]{4,3,2,1,0:T(8,128)(2,1)S(1)} %fusion.126), channel_id=1, source_target_pairs={{0,12},{1,13},{2,14},{3,15},{4,8},{5,9},{6,10},{7,11},{8,4},{9,5},... | collective-permute-start | bytes 983048 | tf_op jit(solution)/shard_map/ppermute | solution.py:215
  625.2 28.5 %collective-permute-start.28 = (bf16[2,2,2,16,1280]{4,3,2,1,0:T(8,128)(2,1)S(1)}, bf16[2,2,2,16,1280]{4,3,2,1,0:T(8,128)(2,1)S(1)}, u32[]{:S(2)}, u32[]{:S(2)}) collective-permute-start(bf16[2,2,2,16,1280]{4,3,2,1,0:T(8,128)(2,1)S(1)} %fusion.123), channel_id=1, source_target_pairs={{0,3},{1,2},{2,1},{3,0},{4,7},{5,6},{6,5},{7,4},{8,11},{9,10},{10,... | collective-permute-start | bytes 983048 | tf_op jit(solution)/shard_map/ppermute | solution.py:215
  627.4 6.6 collective-permute-start.53
  634.0 22.1 %collective-permute-start.37 = (bf16[2,2,2,16,1280]{4,3,2,1,0:T(8,128)(2,1)S(1)}, bf16[2,2,2,16,1280]{4,3,2,1,0:T(8,128)(2,1)S(1)}, u32[]{:S(2)}, u32[]{:S(2)}) collective-permute-start(bf16[2,2,2,16,1280]{4,3,2,1,0:T(8,128)(2,1)S(1)} %fusion.117), channel_id=1, source_target_pairs={{0,1},{1,0},{2,3},{3,2},{4,5},{5,4},{6,7},{7,6},{8,9},{9,8},{10,11... | collective-permute-start | bytes 983048 | tf_op jit(solution)/shard_map/ppermute | solution.py:215
  635.5 5.7 collective-permute-start.54
  641.2 12.7 %collective-permute-start.31 = (bf16[2,2,2,16,1280]{4,3,2,1,0:T(8,128)(2,1)S(1)}, bf16[2,2,2,16,1280]{4,3,2,1,0:T(8,128)(2,1)S(1)}, u32[]{:S(2)}, u32[]{:S(2)}) collective-permute-start(bf16[2,2,2,16,1280]{4,3,2,1,0:T(8,128)(2,1)S(1)} %fusion.125), channel_id=1, source_target_pairs={{0,48},{1,49},{2,50},{3,51},{4,52},{5,53},{6,54},{7,55},{8,56},{9,... | collective-permute-start | bytes 983048 | tf_op jit(solution)/shard_map/ppermute | solution.py:215
  643.7 9.8 %collective-permute-start.55 = (bf16[40,448]{1,0:T(8,128)(2,1)S(1)}, bf16[40,448]{1,0:T(8,128)(2,1)S(1)}, u32[]{:S(2)}, u32[]{:S(2)}) collective-permute-start(bf16[40,448]{1,0:T(8,128)(2,1)S(1)} %fusion.257), channel_id=1, source_target_pairs={{0,48},{1,49},{2,50},{3,51},{4,52},{5,53},{6,54},{7,55},{8,56},{9,... | collective-permute-start | bytes 107528 | tf_op jit(solution)/shard_map/ppermute | solution.py:215
  653.5 7.1 %collective-permute-start.40 = (bf16[2,2,2,16,1280]{4,3,2,1,0:T(8,128)(2,1)S(1)}, bf16[2,2,2,16,1280]{4,3,2,1,0:T(8,128)(2,1)S(1)}, u32[]{:S(2)}, u32[]{:S(2)}) collective-permute-start(bf16[2,2,2,16,1280]{4,3,2,1,0:T(8,128)(2,1)S(1)} %fusion.119), channel_id=1, source_target_pairs={{0,16},{1,17},{2,18},{3,19},{4,20},{5,21},{6,22},{7,23},{8,24},{9,... | collective-permute-start | bytes 983048 | tf_op jit(solution)/shard_map/ppermute | solution.py:215
  654.1 14.9 %collective-permute-start.32 = (bf16[2,2,16,2560]{3,2,1,0:T(8,128)(2,1)S(1)}, bf16[2,2,16,2560]{3,2,1,0:T(8,128)(2,1)S(1)}, u32[]{:S(2)}, u32[]{:S(2)}) collective-permute-start(bf16[2,2,16,2560]{3,2,1,0:T(8,128)(2,1)S(1)} %fusion.130), channel_id=1, source_target_pairs={{0,16},{1,17},{2,18},{3,19},{4,20},{5,21},{6,22},{7,23},{8,24},{9,... | collective-permute-start | bytes 983048 | tf_op jit(solution)/shard_map/ppermute | solution.py:215
  666.0 8.4 %collective-permute-start.41 = (bf16[2,2,16,2560]{3,2,1,0:T(8,128)(2,1)S(1)}, bf16[2,2,16,2560]{3,2,1,0:T(8,128)(2,1)S(1)}, u32[]{:S(2)}, u32[]{:S(2)}) collective-permute-start(bf16[2,2,16,2560]{3,2,1,0:T(8,128)(2,1)S(1)} %fusion.128), channel_id=1, source_target_pairs={{0,48},{1,49},{2,50},{3,51},{4,52},{5,53},{6,54},{7,55},{8,56},{9,... | collective-permute-start | bytes 983048 | tf_op jit(solution)/shard_map/ppermute | solution.py:215
  669.1 6.3 collective-permute-start.33
  674.5 6.6 collective-permute-start.42
  675.4 7.0 %collective-permute-start.34 = (bf16[16,2560]{1,0:T(8,128)(2,1)S(1)}, bf16[16,2560]{1,0:T(8,128)(2,1)S(1)}, u32[]{:S(2)}, u32[]{:S(2)}) collective-permute-start(bf16[16,2560]{1,0:T(8,128)(2,1)S(1)} %fusion.232), channel_id=1, source_target_pairs={{0,1},{1,0},{2,3},{3,2},{4,5},{5,4},{6,7},{7,6},{8,9},{9,8},{10,11... | collective-permute-start | bytes 245768 | tf_op jit(solution)/shard_map/ppermute | solution.py:215
  681.1 5.7 collective-permute-start.43
  (131 other events, 2383.1 us)
Sparse Core Ops, SparseCore 0:
  29.8 123.3 all-gather.2

commit v2 on v1

v2 whole, which is shorter than its diff:
```python
from functools import partial

import jax
import jax.numpy as jnp
from jax import lax
from jax.experimental import pallas as pl
from jax.experimental.pallas import tpu as pltpu
from jax.sharding import PartitionSpec as P

D = 960
HEADS = 15
KV_HEADS = 5
GROUP = HEADS // KV_HEADS
HEAD_DIM = 64
FF = 2560
QD = 960
KVD = 320
OWNERS = 64
SLOT = 15
PADDED = 16
DOWN_ROWS = 40

norm_eps = 1e-05
masked_score = -1e30
rope_base = 10000.0

f32 = jnp.float32
bf16 = jnp.bfloat16


def gray(value):
    return value ^ (value >> 1)


AXIS_SHIFT = {"y": 4, "z": 2, "x": 0}
BITS = (("y", 1), ("y", 0), ("z", 1), ("z", 0), ("x", 1), ("x", 0))


def partner_pairs(bit):
    axis, place = bit
    shift = AXIS_SHIFT[axis]
    pairs = []
    for source in range(OWNERS):
        coordinate = (source >> shift) & 3
        other = gray(gray(coordinate) ^ (1 << place))
        pairs.append((source, source + ((other - coordinate) << shift)))
    return pairs


def owner_of(position):
    me = lax.axis_index("dp")
    owner = 0
    for shift in (4, 2, 0):
        owner = owner + (gray(gray((me >> shift) & 3) ^ ((position >> shift) & 3)) << shift)
    return owner


def dot(left, right):
    return jnp.dot(left, right, preferred_element_type=f32)


def dot_t(left, right):
    return lax.dot_general(left, right, (((1,), (1,)), ((), ())), preferred_element_type=f32)


def spread_matrix():
    row = lax.broadcasted_iota(jnp.int32, (D, OWNERS * PADDED), 0)
    col = lax.broadcasted_iota(jnp.int32, (D, OWNERS * PADDED), 1)
    return ((row == SLOT * (col // PADDED) + col % PADDED) & (col % PADDED < SLOT)).astype(bf16)


def own_spread():
    row = lax.broadcasted_iota(jnp.int32, (OWNERS * PADDED, D), 0)
    col = lax.broadcasted_iota(jnp.int32, (OWNERS * PADDED, D), 1)
    owner = owner_of(row // PADDED)
    return ((col == SLOT * owner + row % PADDED) & (row % PADDED < SLOT)).astype(bf16)


CHUNK = 128
CHUNKS = 8
KV_CHUNKS = 3
PIECES = ((0, 960), (960, 1920), (1920, 2560))
SLABS = 8
VMEM_BYTES = 56 * 2**20


def mm(left, right):
    return lax.dot_general(left, right, (((1,), (0,)), ((), ())), preferred_element_type=f32)


def mm_t(left, right):
    return lax.dot_general(left, right, (((1,), (1,)), ((), ())), preferred_element_type=f32)


def mm_tl(left, right):
    return lax.dot_general(left, right, (((0,), (0,)), ((), ())), preferred_element_type=f32)


def lanes(shape):
    return lax.broadcasted_iota(jnp.int32, shape, len(shape) - 1)


def cut_chunk(value, index):
    width = value.shape[1]
    low = index * CHUNK
    high = min(low + CHUNK, width)
    part = value[:, low:high]
    if high - low < CHUNK:
        part = jnp.concatenate(
            [part, jnp.zeros((value.shape[0], CHUNK - (high - low)), value.dtype)], axis=1
        )
    return part


def turn(value, cosine, sine):
    first = lanes(value.shape) % HEAD_DIM < HEAD_DIM // 2
    swapped = jnp.where(
        first, pltpu.roll(value, CHUNK - HEAD_DIM // 2, 1), pltpu.roll(value, HEAD_DIM // 2, 1)
    )
    return value * cosine + swapped * sine


def doubled(chunk, half):
    other = pltpu.roll(chunk, HEAD_DIM, 1)
    low = lanes(chunk.shape) < HEAD_DIM
    return jnp.where(low, chunk, other) if half == 0 else jnp.where(low, other, chunk)


def only(chunk, half):
    keep = (lanes(chunk.shape) < HEAD_DIM) == (half == 0)
    return jnp.where(keep, chunk, jnp.zeros_like(chunk))


def load_weights(big_ref, down_ref, slabs, down, sems, order):
    copies = {}
    for index in order:
        if index < SLABS:
            copies[index] = pltpu.make_async_copy(
                big_ref.at[:, pl.ds(PADDED * index, PADDED), :], slabs.at[index], sems.at[index]
            )
        else:
            copies[index] = pltpu.make_async_copy(down_ref, down, sems.at[index])
        copies[index].start()
    return copies


def slab(slabs, index, low=0, high=D):
    return slabs[index].reshape(OWNERS * PADDED, D)[:, low:high]


def gate_slab(slabs, piece):
    return slab(slabs, 2 + piece) if piece < 2 else slab(slabs, 6, 0, 640)


def up_slab(slabs, piece):
    return slab(slabs, 4 + piece) if piece < 2 else slab(slabs, 7, 0, 640)


def unit_rows(value):
    inverse = lax.rsqrt(jnp.mean(value * value, axis=-1, keepdims=True) + norm_eps)
    return value * inverse, inverse


def forward_kernel(
    x_ref, cos_ref, sin_ref, allow_ref, live_ref, gains_ref, spread_ref, big_ref, down_ref,
    y_ref, q_ref, k_ref, v_ref, p_ref, o_ref, m_ref, g0_ref, g1_ref, g2_ref, u0_ref, u1_ref, u2_ref,
    slabs, down, sems,
):
    copies = load_weights(big_ref, down_ref, slabs, down, sems, (0, 6, 7, 1, 2, 4, 3, 5, 8))
    cosine, sine = cos_ref[...], sin_ref[...]
    allowed = allow_ref[...] > 0
    spread = spread_ref[...]
    h = x_ref[...].astype(f32)
    n1, _ = unit_rows(h)
    a = (n1 * gains_ref[0:1, :]).astype(bf16)
    a_wide = mm(a, spread).astype(bf16)
    copies[0].wait()
    q_all = mm(a_wide, slab(slabs, 0))
    copies[6].wait()
    k_all = mm(a_wide, slab(slabs, 6, 640, 960))
    copies[7].wait()
    v_all = mm(a_wide, slab(slabs, 7, 640, 960))
    keys, values = [], []
    for index in range(KV_CHUNKS):
        k_chunk = turn(cut_chunk(k_all, index), cosine, sine)
        v_chunk = cut_chunk(v_all, index)
        k_ref[index] = k_chunk.astype(bf16)
        v_ref[index] = v_chunk.astype(bf16)
        for half in range(2):
            keys.append(doubled(k_chunk, half).astype(bf16))
            values.append(doubled(v_chunk, half).astype(bf16))
    mixed = []
    for index in range(CHUNKS):
        q_chunk = turn(cut_chunk(q_all, index), cosine, sine).astype(bf16)
        q_ref[index] = q_chunk
        total = None
        for half in range(2):
            head = 2 * index + half
            if head >= HEADS:
                continue
            s = mm_t(only(q_chunk, half), keys[head // GROUP]) * HEAD_DIM**-0.5
            s = jnp.where(allowed, s, masked_score)
            e = jnp.exp(s - jnp.max(s, axis=-1, keepdims=True))
            p = e / jnp.sum(e, axis=-1, keepdims=True)
            p_ref[head] = p
            part = mm(p.astype(bf16), only(values[head // GROUP], half))
            total = part if total is None else total + part
        mixed.append(total)
    o = jnp.concatenate(mixed, axis=1)[:, :QD].astype(bf16)
    o_ref[...] = o
    o_wide = mm(o, spread).astype(bf16)
    copies[1].wait()
    m = h + mm(o_wide, slab(slabs, 1))
    m_ref[...] = m
    n2, _ = unit_rows(m)
    b = (n2 * gains_ref[1:2, :]).astype(bf16)
    b_wide = mm(b, spread).astype(bf16)
    hiddens = []
    for piece, (g_ref, u_ref) in enumerate(((g0_ref, u0_ref), (g1_ref, u1_ref), (g2_ref, u2_ref))):
        if piece < 2:
            copies[2 + piece].wait()
            copies[4 + piece].wait()
        gate = mm(b_wide, gate_slab(slabs, piece))
        up = mm(b_wide, up_slab(slabs, piece))
        g_ref[...] = gate
        u_ref[...] = up
        hiddens.append((gate * lax.logistic(gate) * up).astype(bf16))
    copies[8].wait()
    total = m
    for (low, high), hidden in zip(PIECES, hiddens):
        total = total + mm(hidden, down[low:high, :])
    y_ref[...] = (total * live_ref[...]).astype(bf16)


def narrow(value, spread):
    high = value.astype(bf16)
    low = (value - high.astype(f32)).astype(bf16)
    return mm_t(high, spread) + mm_t(low, spread)


def norm_grad(grad, normal, inverse, gain):
    scaled = grad * gain
    inner = jnp.mean(scaled * normal, axis=-1, keepdims=True)
    return inverse * (scaled - normal * inner)


def feed_forward_back_kernel(
    top_ref, m_ref, g0_ref, g1_ref, g2_ref, u0_ref, u1_ref, u2_ref,
    live_ref, gains_ref, spread_ref, big_ref, down_ref,
    dm_ref, low_ref, d3_ref, dg0_ref, dg1_ref, dg2_ref, du0_ref, du1_ref, du2_ref,
    dgain_ref, b_ref, h0_ref, h1_ref, h2_ref,
    slabs, down, sems,
):
    copies = load_weights(big_ref, down_ref, slabs, down, sems, (8, 2, 4, 3, 5, 6, 7))
    spread = spread_ref[...]
    gain_f = gains_ref[1:2, :]
    d3 = top_ref[...].astype(f32) * live_ref[...]
    d3_low = d3.astype(bf16)
    d3_ref[...] = d3_low
    n2, r2 = unit_rows(m_ref[...])
    b_ref[...] = (n2 * gain_f).astype(bf16)
    copies[8].wait()
    wide = jnp.zeros((d3.shape[0], OWNERS * PADDED), f32)
    refs = (
        (g0_ref, u0_ref, dg0_ref, du0_ref, h0_ref),
        (g1_ref, u1_ref, dg1_ref, du1_ref, h1_ref),
        (g2_ref, u2_ref, dg2_ref, du2_ref, h2_ref),
    )
    for piece, (g_ref, u_ref, dg_ref, du_ref, hid_ref) in enumerate(refs):
        low, high = PIECES[piece]
        dhidden = mm_t(d3_low, down[low:high, :])
        gate, up = g_ref[...], u_ref[...]
        sig = lax.logistic(gate)
        act = gate * sig
        hid_ref[...] = (act * up).astype(bf16)
        dg = (dhidden * up * sig * (1.0 + gate * (1.0 - sig))).astype(bf16)
        du = (dhidden * act).astype(bf16)
        dg_ref[...] = dg
        du_ref[...] = du
        if piece < 2:
            copies[2 + piece].wait()
            copies[4 + piece].wait()
        else:
            copies[6].wait()
            copies[7].wait()
        wide = wide + mm_t(dg, gate_slab(slabs, piece)) + mm_t(du, up_slab(slabs, piece))
    db = narrow(wide, spread)
    dgain_ref[...] = jnp.sum(db * n2, axis=0, keepdims=True)
    dm = d3 + norm_grad(db, n2, r2, gain_f)
    dm_ref[...] = dm
    low_ref[...] = dm.astype(bf16)


def attention_back_kernel(
    x_ref, dm_ref, low_ref, q_ref, k_ref, v_ref, p_ref,
    cos_ref, sin_ref, gains_ref, spread_ref, big_ref,
    dh_ref, dq_ref, dk_ref, dv_ref, dgain_ref, a_ref,
    slabs, sems,
):
    copies = load_weights(big_ref, None, slabs, None, sems, (1, 0, 6, 7))
    cosine, sine = cos_ref[...], sin_ref[...]
    spread = spread_ref[...]
    gain_a = gains_ref[0:1, :]
    copies[1].wait()
    do = mm_t(mm_t(low_ref[...], slab(slabs, 1)).astype(bf16), spread).astype(bf16)
    keys, values = [], []
    for index in range(KV_CHUNKS):
        k_chunk, v_chunk = k_ref[index].astype(f32), v_ref[index].astype(f32)
        for half in range(2):
            keys.append(doubled(k_chunk, half).astype(bf16))
            values.append(doubled(v_chunk, half).astype(bf16))
    dk_sums, dv_sums = [None] * KV_HEADS, [None] * KV_HEADS
    dq_parts = []
    for index in range(CHUNKS):
        do_chunk = cut_chunk(do, index)
        q_chunk = q_ref[index]
        total = None
        for half in range(2):
            head = 2 * index + half
            if head >= HEADS:
                continue
            group = head // GROUP
            do_head, q_head = only(do_chunk, half), only(q_chunk, half)
            p = p_ref[head]
            dp = mm_t(do_head, values[group])
            dv = mm_tl(p.astype(bf16), do_head)
            ds = (p * (dp - jnp.sum(p * dp, axis=-1, keepdims=True))).astype(bf16)
            dk = mm_tl(ds, q_head)
            part = mm(ds, only(keys[group], half))
            total = part if total is None else total + part
            dk_sums[group] = dk if dk_sums[group] is None else dk_sums[group] + dk
            dv_sums[group] = dv if dv_sums[group] is None else dv_sums[group] + dv
        dq_parts.append(turn(total * HEAD_DIM**-0.5, cosine, -sine))
    dq = jnp.concatenate(dq_parts, axis=1)[:, :QD].astype(bf16)
    low_lanes = lanes((do.shape[0], CHUNK)) < HEAD_DIM
    dk_parts, dv_parts = [], []
    for index in range(KV_CHUNKS):
        both = []
        for sums in (dk_sums, dv_sums):
            halves = []
            for half in range(2):
                group = 2 * index + half
                if group < KV_HEADS:
                    halves.append(sums[group] + pltpu.roll(sums[group], HEAD_DIM, 1))
                else:
                    halves.append(jnp.zeros_like(sums[0]))
            both.append(jnp.where(low_lanes, halves[0], halves[1]))
        dk_parts.append(turn(both[0] * HEAD_DIM**-0.5, cosine, -sine))
        dv_parts.append(both[1])
    dk = jnp.concatenate(dk_parts, axis=1)[:, :KVD].astype(bf16)
    dv = jnp.concatenate(dv_parts, axis=1)[:, :KVD].astype(bf16)
    dq_ref[...] = dq
    dk_ref[...] = dk
    dv_ref[...] = dv
    h = x_ref[...].astype(f32)
    n1, r1 = unit_rows(h)
    a_ref[...] = (n1 * gain_a).astype(bf16)
    copies[0].wait()
    copies[6].wait()
    copies[7].wait()
    wide = (
        mm_t(dq, slab(slabs, 0))
        + mm_t(dk, slab(slabs, 6, 640, 960))
        + mm_t(dv, slab(slabs, 7, 640, 960))
    )
    da = narrow(wide, spread)
    dgain_ref[...] = jnp.sum(da * n1, axis=0, keepdims=True)
    dh = dm_ref[...] + norm_grad(da, n1, r1, gain_a)
    dh_ref[...] = dh.astype(bf16)


def takes(microseconds):
    return pl.CostEstimate(
        flops=int(microseconds * 1.1e9), bytes_accessed=int(microseconds * 1e6), transcendentals=0
    )


def specs(count, anywhere=0):
    return [pl.BlockSpec(memory_space=pltpu.VMEM)] * count + [
        pl.BlockSpec(memory_space=pl.ANY)
    ] * anywhere


def weight_scratch():
    return [
        pltpu.VMEM((SLABS, OWNERS, PADDED, D), bf16),
        pltpu.VMEM((FF, D), bf16),
        pltpu.SemaphoreType.DMA((SLABS + 1,)),
    ]


def shapes(entries):
    return [jax.ShapeDtypeStruct(shape, kind) for shape, kind in entries]


def forward(x, tables, gains, spread, big, down):
    cosine, sine, allowed, live = tables
    rows = x.shape[0]
    widths = [high - low for low, high in PIECES]
    out = shapes(
        [
            ((rows, D), bf16),
            ((CHUNKS, rows, CHUNK), bf16),
            ((KV_CHUNKS, rows, CHUNK), bf16),
            ((KV_CHUNKS, rows, CHUNK), bf16),
            ((HEADS, rows, rows), f32),
            ((rows, QD), bf16),
            ((rows, D), f32),
        ]
        + [((rows, width), f32) for width in widths * 2]
    )
    return pl.pallas_call(
        forward_kernel,
        out_shape=out,
        in_specs=specs(7, 2),
        out_specs=specs(len(out)),
        scratch_shapes=weight_scratch(),
        compiler_params=pltpu.CompilerParams(vmem_limit_bytes=VMEM_BYTES),
        name="layer_forward",
        cost_estimate=takes(13),
    )(x, cosine, sine, allowed, live, gains, spread, big, down)


def feed_forward_back(top, saved, tables, gains, spread, big, down):
    live = tables[3]
    rows = top.shape[0]
    widths = [high - low for low, high in PIECES]
    out = shapes(
        [((rows, D), f32), ((rows, D), bf16), ((rows, D), bf16)]
        + [((rows, width), bf16) for width in widths * 2]
        + [((1, D), f32), ((rows, D), bf16)]
        + [((rows, width), bf16) for width in widths]
    )
    return pl.pallas_call(
        feed_forward_back_kernel,
        out_shape=out,
        in_specs=specs(11, 2),
        out_specs=specs(len(out)),
        scratch_shapes=weight_scratch(),
        compiler_params=pltpu.CompilerParams(vmem_limit_bytes=VMEM_BYTES),
        name="feed_forward_back",
        cost_estimate=takes(14),
    )(top, *saved[5:], live, gains, spread, big, down)


def attention_back(x, dm, dm_low, saved, tables, gains, spread, big):
    cosine, sine, _, _ = tables
    rows = x.shape[0]
    out = shapes(
        [((rows, D), bf16), ((rows, QD), bf16), ((rows, KVD), bf16), ((rows, KVD), bf16)]
        + [((1, D), f32), ((rows, D), bf16)]
    )
    scratch = weight_scratch()
    return pl.pallas_call(
        attention_back_kernel,
        out_shape=out,
        in_specs=specs(11, 1),
        out_specs=specs(len(out)),
        scratch_shapes=[scratch[0], scratch[2]],
        compiler_params=pltpu.CompilerParams(vmem_limit_bytes=VMEM_BYTES),
        name="attention_back",
        cost_estimate=takes(11.5),
    )(x, dm, dm_low, *saved[:4], cosine, sine, gains, spread, big)


def tables_of(starts):
    micro, rows = starts.shape
    local = jnp.arange(rows, dtype=jnp.int32)
    live = (starts <= local).reshape(-1)
    position = jnp.where(starts <= local, local - starts, 0).astype(f32).reshape(-1, 1)
    lane = jnp.arange(CHUNK, dtype=jnp.int32)
    turn_index = (lane % (HEAD_DIM // 2)).astype(f32)
    angles = position * rope_base ** (-2.0 * turn_index / HEAD_DIM)
    sign = jnp.where(lane % HEAD_DIM < HEAD_DIM // 2, -1.0, 1.0).astype(f32)
    row = jnp.arange(micro * rows, dtype=jnp.int32)
    begin = starts.reshape(-1, 1)
    column = row[None, :]
    same = (row[:, None] // rows) == (column // rows)
    inside = (column % rows >= begin) & (column <= row[:, None])
    allowed = (same & inside) | (row[:, None] == column)
    return jnp.cos(angles), jnp.sin(angles) * sign, allowed.astype(f32), live.astype(f32)[:, None]


STREAM_KINDS = (("a", "gain"), ("b",), ("b",), ("h0", "h1"), ("o", "h2"))
STREAM_RIGHTS = (14, 20, 20, 8, 16)
STREAM_CHUNKS = (14, 20, 20, 16, 12)
LEFT_ROWS = OWNERS // 2 * PADDED


def rotations(place, then):
    axes = "yzx"
    result = []
    for turned in (axes[start:] + axes[:start] for start in range(3)):
        result.append(
            tuple((axis, place) for axis in turned) + tuple((axis, then) for axis in turned)
        )
    return result


HIGH_FIRST, LOW_FIRST = rotations(1, 0), rotations(0, 1)
ORDERS = (HIGH_FIRST[0], LOW_FIRST[0], LOW_FIRST[1], HIGH_FIRST[1], HIGH_FIRST[2])
GROUPS = ((0, 3, 4), (1, 2))


def split_bit(value, dim, bits):
    shape = value.shape[1:]
    view = value.reshape((2**dim, 2, 2 ** (bits - 1 - dim)) + shape)
    return [view[:, index].reshape((2 ** (bits - 1),) + shape) for index in (0, 1)]


def chunks_of(value):
    count = (value.shape[1] + CHUNK - 1) // CHUNK
    return [cut_chunk(value, index) for index in range(count)]


def write_stream(stream, lefts, rights, keep_ref, pack_ref):
    rows = rights[0].shape[0]
    dim = BITS.index(ORDERS[stream][0])
    base = 0
    for index, left in enumerate(lefts):
        kept, sent = split_bit(left, dim, 6)
        keep_ref[index] = kept
        pack_ref[base : base + LEFT_ROWS, :] = sent.reshape(LEFT_ROWS, rows)
        base += LEFT_ROWS
    for chunk in rights:
        pack_ref[base : base + rows, :] = chunk
        base += rows


def in_order(mine, value):
    return mm_t(mine, value).astype(bf16).reshape(OWNERS, PADDED, value.shape[0])


def late_operand_kernel(
    mine_ref, a_ref, attn_ref, ffn_ref, dq_ref, dk_ref, dv_ref, keep_ref, pack_ref
):
    mine = mine_ref[...]
    rows = a_ref.shape[0]
    gain = jnp.concatenate([attn_ref[...], ffn_ref[...], jnp.zeros((rows - 2, D), f32)], axis=0)
    lefts = in_order(mine, a_ref[...]), in_order(mine, gain.astype(bf16))
    dq, dk, dv = dq_ref[...], dk_ref[...], dv_ref[...]
    tail = jnp.concatenate([dq[:, 896:], dk[:, 256:]], axis=1)
    identity = lax.broadcasted_iota(jnp.int32, (rows, CHUNK), 0) == lanes((rows, CHUNK))
    rights = chunks_of(dq)[:7] + chunks_of(dk)[:2] + [tail] + chunks_of(dv)
    write_stream(0, lefts, rights + [identity.astype(f32).astype(bf16)], keep_ref, pack_ref)


def early_operand_kernel(
    owner_ref, mine_ref, b_ref, o_ref, h0_ref, h1_ref, h2_ref, dm_ref, d3_ref,
    dg0_ref, dg1_ref, dg2_ref, du0_ref, du1_ref, du2_ref,
    *rest,
):
    keeps, packs = rest[:4], rest[4:8]
    turned, lefts = rest[8:]
    mine = mine_ref[...]
    rows = b_ref.shape[0]

    hidden = jnp.concatenate([h0_ref[...], h1_ref[...], h2_ref[...]], axis=1).astype(f32)
    turned[...] = hidden.T.reshape(OWNERS, DOWN_ROWS, rows)

    @pl.loop(0, OWNERS)
    def _(place):
        block = turned[owner_ref[place]]
        lefts[0, place] = block[0:16].astype(bf16)
        lefts[1, place] = block[16:32].astype(bf16)
        lefts[2, place] = jnp.concatenate(
            [block[32:40], jnp.zeros((8, rows), f32)], axis=0
        ).astype(bf16)

    b = in_order(mine, b_ref[...])
    o = in_order(mine, o_ref[...])
    dg = jnp.concatenate([dg0_ref[...], dg1_ref[...], dg2_ref[...]], axis=1)
    du = jnp.concatenate([du0_ref[...], du1_ref[...], du2_ref[...]], axis=1)
    d3, dm = chunks_of(d3_ref[...]), chunks_of(dm_ref[...])
    write_stream(1, (b,), chunks_of(dg), keeps[0], packs[0])
    write_stream(2, (b,), chunks_of(du), keeps[1], packs[1])
    write_stream(3, (lefts[0], lefts[1]), d3, keeps[2], packs[2])
    write_stream(4, (o, lefts[2]), dm + d3, keeps[3], packs[3])


def operand_shapes(streams, rows):
    return shapes(
        [((len(STREAM_KINDS[s]), OWNERS // 2, PADDED, rows), bf16) for s in streams]
        + [
            ((len(STREAM_KINDS[s]) * LEFT_ROWS + STREAM_RIGHTS[s] * rows, CHUNK), bf16)
            for s in streams
        ]
    )


def early_operands(mine, b, o, hidden, dm_low, d3, dg, du):
    rows = b.shape[0]
    out = operand_shapes((1, 2, 3, 4), rows)
    owners = owner_of(jnp.arange(OWNERS, dtype=jnp.int32))
    result = pl.pallas_call(
        early_operand_kernel,
        out_shape=out,
        in_specs=[pl.BlockSpec(memory_space=pltpu.SMEM)] + specs(14),
        out_specs=specs(len(out)),
        scratch_shapes=[
            pltpu.VMEM((OWNERS, DOWN_ROWS, rows), f32),
            pltpu.VMEM((3, OWNERS, PADDED, rows), bf16),
        ],
        compiler_params=pltpu.CompilerParams(vmem_limit_bytes=VMEM_BYTES),
        name="early_operands",
        cost_estimate=takes(7),
    )(owners, mine, b, o, *hidden, dm_low, d3, *dg, *du)
    return result[:4], result[4:]


def late_operands(mine, a, dattn, dffn, dq, dk, dv):
    out = operand_shapes((0,), a.shape[0])
    return pl.pallas_call(
        late_operand_kernel,
        out_shape=out,
        in_specs=specs(7),
        out_specs=specs(2),
        compiler_params=pltpu.CompilerParams(vmem_limit_bytes=VMEM_BYTES),
        name="late_operands",
        cost_estimate=takes(4),
    )(mine, a, dattn, dffn, dq, dk, dv)


def product_kernel(streams, *refs):
    count = len(streams)
    keeps, packs, others = (
        dict(zip(streams, refs[count * part : count * (part + 1)])) for part in range(3)
    )
    outs = {s: refs[3 * count + 2 * i : 3 * count + 2 * i + 2] for i, s in enumerate(streams)}
    step = pl.program_id(0)

    def left_of(stream, kind):
        kept = keeps[stream][kind].reshape(LEFT_ROWS, CHUNK)
        window = pl.ds(kind * LEFT_ROWS, LEFT_ROWS)
        return jnp.concatenate([kept, others[stream][window, :]], axis=1)

    def right_of(stream, chunk):
        start = len(STREAM_KINDS[stream]) * LEFT_ROWS + chunk * CHUNK
        if not isinstance(start, int):
            start = pl.multiple_of(start, CHUNK)
        window = pl.ds(start, CHUNK)
        return jnp.concatenate([packs[stream][window, :], others[stream][window, :]], axis=0)

    def right_pair(stream, first, second):
        return jnp.concatenate([right_of(stream, first), right_of(stream, second)], axis=1)

    def blocks_of(value):
        return value.reshape(OWNERS // 2, PADDED, CHUNK)

    def store(stream, place, value):
        dim = [bit for bit in BITS if bit != ORDERS[stream][0]].index(ORDERS[stream][1])
        kept, sent = split_bit(value.astype(bf16), dim, 5)
        outs[stream][0][place] = kept
        outs[stream][1][place] = sent

    def usual(stream, kind, first):
        value = mm(left_of(stream, kind), right_pair(stream, first, first + 1))
        store(stream, 0, blocks_of(value[:, :CHUNK]))
        store(stream, 1, blocks_of(value[:, CHUNK:]))

    def short_rows(stream, kind, first):
        value = mm(left_of(stream, kind), right_pair(stream, first, first + 4))
        parts = [blocks_of(part)[:, :8] for part in (value[:, :CHUNK], value[:, CHUNK:])]
        return jnp.concatenate(parts, axis=1)

    def when(condition, action):
        pl.when(condition)(action)

    if 0 in streams:
        when(step < 6, lambda: usual(0, 0, 2 * step))

        @pl.when(step == 6)
        def _():
            store(0, 0, blocks_of(mm(left_of(0, 0), right_of(0, 12))))
            store(0, 1, blocks_of(mm(left_of(0, 1), right_of(0, 13))))

    if 1 in streams:
        usual(1, 0, 2 * step)
    if 2 in streams:
        usual(2, 0, 2 * step)
    if 3 in streams:
        when(step < 4, lambda: usual(3, 0, 2 * step))
        when(step >= 4, lambda: usual(3, 1, 2 * step - 8))
    if 4 in streams:
        when(step < 4, lambda: usual(4, 0, 2 * step))

        @pl.when((step >= 4) & (step < 6))
        def _():
            for place in range(2):
                store(4, place, short_rows(4, 1, 8 + 2 * (step - 4) + place))


def products(streams, keeps, packs, others):
    out, out_specs = [], []
    for stream in streams:
        last = STREAM_CHUNKS[stream] // 2 - 1
        for _ in range(2):
            out.append(((STREAM_CHUNKS[stream], OWNERS // 4, PADDED, CHUNK), bf16))
            out_specs.append(
                pl.BlockSpec(
                    (2, OWNERS // 4, PADDED, CHUNK),
                    lambda step, last=last: (jnp.minimum(step, last), 0, 0, 0),
                )
            )
    result = pl.pallas_call(
        partial(product_kernel, streams),
        grid=(max(STREAM_CHUNKS[stream] for stream in streams) // 2,),
        out_shape=shapes(out),
        in_specs=specs(3 * len(streams)),
        out_specs=out_specs,
        compiler_params=pltpu.CompilerParams(vmem_limit_bytes=VMEM_BYTES),
        name="grad_products",
        cost_estimate=takes(sum(STREAM_CHUNKS[stream] for stream in streams) * 0.2),
    )(*keeps, *packs, *others)
    return list(result[0::2]), list(result[1::2])


def together(values):
    return list(lax.optimization_barrier(tuple(values)))


def send(values, bits):
    return together([lax.ppermute(v, "dp", partner_pairs(b)) for v, b in zip(values, bits)])


def halved(kept, arrived, dim):
    size = kept.shape[1]
    view = (kept.shape[0], 2**dim, 2, size >> (dim + 1)) + kept.shape[2:]
    flat = (kept.shape[0], size // 2) + kept.shape[2:]
    first, second = kept.reshape(view), arrived.reshape(view)
    return tuple(
        (first[:, :, index].astype(f32) + second[:, :, index].astype(f32))
        .astype(bf16)
        .reshape(flat)
        for index in (0, 1)
    )


def exchanged(streams, packs):
    return send(packs, [ORDERS[stream][0] for stream in streams])


def three_steps(streams, keeps, packs, others):
    orders = [ORDERS[stream] for stream in streams]
    kept, sent = products(streams, keeps, packs, others)
    arrived = send(sent, [order[1] for order in orders])
    for index, order in enumerate(orders):
        left = [bit for bit in BITS if bit not in order[:2]]
        kept[index], sent[index] = halved(kept[index], arrived[index], left.index(order[2]))
    return kept, send(sent, [order[2] for order in orders])


def last_steps(parts):
    kept, sent, rest = [], [], []
    for members, (keeps, arrived) in zip(GROUPS, parts):
        order = ORDERS[members[0]]
        left = [bit for bit in BITS if bit not in order[:3]]
        halves = [halved(k, a, left.index(order[3])) for k, a in zip(keeps, arrived)]
        kept.append(jnp.concatenate([half[0] for half in halves], axis=0))
        sent.append(jnp.concatenate([half[1] for half in halves], axis=0))
        rest.append((left, order[3:]))
    for step in range(3):
        arrived = send(sent, [order[step] for _, order in rest])
        for group, (left, order) in enumerate(rest):
            left.remove(order[step])
            if step < 2:
                dim = left.index(order[step + 1])
                kept[group], sent[group] = halved(kept[group], arrived[group], dim)
    return kept, arrived


def result_kernel(
    kept0_ref, kept1_ref, came0_ref, came1_ref,
    query_ref, key_ref, value_ref, output_ref, gate_ref, up_ref, down_ref, attn_ref, ffn_ref,
):
    def block(group, index):
        kept, came = ((kept0_ref, came0_ref), (kept1_ref, came1_ref))[group]
        return kept[index, 0].astype(f32) + came[index, 0].astype(f32)

    def put(ref, low, high, value, column):
        width = min(CHUNK, ref.shape[-1] - column)
        value = value[: high - low, :width]
        if len(ref.shape) == 3:
            ref[low:high, 0, column : column + width] = value
        else:
            ref[low:high, column : column + width] = value

    half = HEAD_DIM
    for index in range(7):
        put(query_ref, 0, SLOT, block(0, index), CHUNK * index)
    for index in range(2):
        put(key_ref, 0, SLOT, block(0, 7 + index), CHUNK * index)
    tail = block(0, 9)
    put(query_ref, 0, SLOT, tail, 896)
    put(key_ref, 0, SLOT, tail[:, half:], 256)
    for index in range(3):
        put(value_ref, 0, SLOT, block(0, 10 + index), CHUNK * index)
    gains = block(0, 13)
    eye = (lax.broadcasted_iota(jnp.int32, (8, CHUNK), 0) == lanes((8, CHUNK))).astype(f32)
    turned = lax.dot_general(
        eye, gains, (((1,), (1,)), ((), ())),
        preferred_element_type=f32, precision=lax.Precision.HIGHEST,
    )
    attn_ref[...] = turned[0:1, :SLOT]
    ffn_ref[...] = turned[1:2, :SLOT]
    for index in range(8):
        put(down_ref, 0, 16, block(0, 14 + index), CHUNK * index)
        put(down_ref, 16, 32, block(0, 22 + index), CHUNK * index)
        put(output_ref, 0, SLOT, block(0, 30 + index), CHUNK * index)
    for index in range(4):
        both = block(0, 38 + index)
        put(down_ref, 32, 40, both[:8], CHUNK * index)
        put(down_ref, 32, 40, both[8:], CHUNK * (index + 4))
    for index in range(20):
        put(gate_ref, 0, SLOT, block(1, index), CHUNK * index)
        put(up_ref, 0, SLOT, block(1, 20 + index), CHUNK * index)


def weight_results(kept, came):
    wide = [(SLOT, 1, width) for width in (QD, KVD, KVD, D, FF, FF)]
    out = shapes([(shape, f32) for shape in wide + [(DOWN_ROWS, D), (1, SLOT), (1, SLOT)]])
    result = pl.pallas_call(
        result_kernel,
        out_shape=out,
        in_specs=specs(4),
        out_specs=specs(len(out)),
        name="weight_results",
        cost_estimate=takes(3),
    )(*kept, *came)
    slots = tuple(value.transpose(1, 0, 2) for value in result[:6])
    return slots + (result[6][None],) + tuple(result[7:])


def pack_kernel(q_ref, k_ref, v_ref, o_ref, g_ref, u_ref, d_ref, gain_ref, out_ref):
    blank = jnp.zeros((PADDED - SLOT, D), bf16)
    g, u = g_ref[0], u_ref[0]
    plain = (
        q_ref[0],
        o_ref[0],
        g[:, :960],
        g[:, 960:1920],
        u[:, :960],
        u[:, 960:1920],
        jnp.concatenate([g[:, 1920:], k_ref[0]], axis=1),
        jnp.concatenate([u[:, 1920:], v_ref[0]], axis=1),
    )
    for index, value in enumerate(plain):
        last = gain_ref[...] if index == 0 else blank
        full = jnp.concatenate([value.astype(f32), last.astype(f32)], axis=0)
        out_ref[0, PADDED * index : PADDED * (index + 1), :] = full.astype(bf16)
    out_ref[0, PADDED * SLABS :, :] = d_ref[0]


def packed_weights(w_query, w_key, w_value, w_output, w_gate, w_up, w_down, attn_gain, ffn_gain):
    gains = jnp.concatenate([attn_gain, ffn_gain], axis=1)
    gain_row = jnp.pad(gains, ((0, 0), (0, D - gains.shape[1])))
    return pl.pallas_call(
        pack_kernel,
        out_shape=jax.ShapeDtypeStruct((1, PADDED * SLABS + DOWN_ROWS, D), bf16),
        in_specs=specs(8),
        out_specs=pl.BlockSpec(memory_space=pltpu.VMEM),
        name="pack_weights",
        cost_estimate=takes(2),
    )(w_query, w_key, w_value, w_output, w_gate, w_up, w_down, gain_row)


def body(inputs, starts, cotangent, *weights):
    section = lax.axis_index("section")
    micro, rows = starts.shape
    everything = lax.all_gather(packed_weights(*weights), "dp", axis=0, tiled=True)
    down = everything[:, SLABS * PADDED :].reshape(FF, D)
    all_gains = everything[:, SLOT, : 2 * SLOT].astype(f32)
    all_gains = jnp.stack([all_gains[:, :SLOT].reshape(D), all_gains[:, SLOT:].reshape(D)])
    spread = spread_matrix()
    mine = own_spread()
    tables = tables_of(starts)
    first_in = inputs.reshape(micro * rows, D)
    top = cotangent.reshape(micro * rows, D)
    shared = (tables, all_gains, spread, everything)

    made = forward(first_in, *shared, down)[0]
    arrived = lax.ppermute(made, "section", [(0, 1)])
    source = jnp.where(section == 0, first_in, arrived)
    result, *saved = forward(source, *shared, down)

    dm, dm_low = feed_forward_back(top, saved, *shared, down)[:2]
    back = attention_back(source, dm, dm_low, saved, *shared)[0]
    returned = lax.ppermute(back, "section", [(1, 0)])
    upstream = jnp.where(section == 1, top, returned)

    ffn = feed_forward_back(upstream, saved, *shared, down)
    dm, dm_low, d3, dffn, b, hidden = ffn[0], ffn[1], ffn[2], ffn[9], ffn[10], ffn[11:14]
    keeps, packs = early_operands(mine, b, saved[4], hidden, dm_low, d3, ffn[3:6], ffn[6:9])
    dm, dm_low, *packs = together([dm, dm_low, *packs])
    others = exchanged((1, 2, 3, 4), packs)
    grad_rows, dq, dk, dv, dattn, a = attention_back(source, dm, dm_low, saved, *shared)
    a, *others = together([a, *others])
    late_keep, late_pack = late_operands(mine, a, dattn, dffn, dq, dk, dv)
    last = exchanged((0,), [late_pack])

    gate_up = three_steps((1, 2), keeps[:2], packs[:2], others[:2])
    down_out = three_steps((3, 4), keeps[2:], packs[2:], others[2:])
    query = three_steps((0,), [late_keep], [late_pack], last)
    first_group = (query[0] + down_out[0], query[1] + down_out[1])
    sums = weight_results(*last_steps((first_group, gate_up)))
    rows_out = (result.reshape(1, micro, rows, D), grad_rows.reshape(1, micro, rows, D))
    return rows_out + sums


def solution(mesh):
    split = P("section", "dp", None)
    return jax.shard_map(
        body,
        mesh=mesh,
        in_specs=(P(None, "dp", None), P(None, "dp"), P(None, "dp", None))
        + (split,) * 7
        + (P("section", "dp"),) * 2,
        out_specs=(P("section", None, "dp", None),) * 2
        + (split,) * 7
        + (P("section", "dp"),) * 2,
        check_vma=False,
    )
```

time: 709 us -> 372 us (0.52)
  matrix products: 147 us -> 0 us
  local copies, waits for them, and re-layouts: 152 us -> 8.97 us
  Pallas kernels: 0 us -> 113 us
  waiting for transfers between devices: 268 us -> 183 us
  starting transfers between devices: 66.3 us -> 29.6 us
  other arithmetic: 45.4 us -> 15.9 us
    dot_general x77 -> x0, matrix products: 142 us -> none  [the longest x41 78.1 us: dot(): return jnp.dot(left, right, preferred_element_type=f32)]
    pallas_call x0 -> x13, Pallas kernels: none -> 113 us  [the longest x2 28.1 us: feed_forward_back(): pl.pallas_call(feed_forward_back_kernel, out_shape=out, in_specs=specs(11...]
    ppermute x54 -> x21, waiting for transfers between devices: 156 us -> 63.2 us  [send(): lax.ppermute(v, 'dp', partner_pairs(b))]
    concatenate x11 -> x0, local copies, waits for them, and re-layouts: 48.2 us -> none  [the longest x1 18.6 us: body(): packed = jnp.concatenate(pieces + [w_down[0]], axis=0)[None]]
    ppermute x54 -> x21, starting transfers between devices: 62.5 us -> 26.1 us  [send(): lax.ppermute(v, 'dp', partner_pairs(b))]
    slice x20 -> x2, local copies, waits for them, and re-layouts: 36.6 us -> 5.56 us  [the longest x1 5.48 us: body(): down = everything[:, SLABS * PADDED:].reshape(FF, D)]
    convert_element_type x19 -> x7, local copies, waits for them, and re-layouts: 27.7 us -> 1.12 us  [the longest x1 0.76 us: tables_of(): live.astype(f32)[:, None]]
    convert_element_type x61 -> x21, other arithmetic: 28.2 us -> 9.75 us  [the longest x16 4.37 us: halved(): return tuple(((first[:, :, index].astype(f32) + second[:, :, index].astyp...]
  transfers between devices with their start and end apart: 57 -> 24, of which waited for: 30 -> 16; matrix products, arithmetic and copies ran while one was open for 12% -> 3% of each run, Pallas kernels for 0% -> 9%
where the time goes in v2:
time: 372 us; the launch traced here: 365 us
  waiting for transfers between devices  183 us (49%)
  Pallas kernels  113 us (30%)
  starting transfers between devices  29.6 us (8%)
  other arithmetic  15.9 us (4%)
  between operations  14.9 us (4%)
  local copies, waits for them, and re-layouts  8.97 us (2%)
    all_gather x1, waiting for transfers between devices, body(): lax.all_gather(packed_weights(*weights), 'dp', axis=0, tiled=True)  119 us
    ppermute x21, waiting for transfers between devices, send(): lax.ppermute(v, 'dp', partner_pairs(b))  63.2 us
    pallas_call x2, Pallas kernels, feed_forward_back(): pl.pallas_call(feed_forward_back_kernel, out_shape=out, in_specs=specs(11...  28.1 us
    pallas_call x2, Pallas kernels, forward(): pl.pallas_call(forward_kernel, out_shape=out, in_specs=specs(7, 2), out_s...  26.8 us
    ppermute x21, starting transfers between devices, send(): lax.ppermute(v, 'dp', partner_pairs(b))  26.1 us
    pallas_call x2, Pallas kernels, attention_back(): pl.pallas_call(attention_back_kernel, out_shape=out, in_specs=specs(11, 1...  23.1 us
    pallas_call x3, Pallas kernels, products(): pl.pallas_call(partial(product_kernel, streams), grid=(max((STREAM_CHUNKS...  20.3 us
  transfers between devices with their start and end apart: 24, of which 16 were waited for; matrix products, arithmetic and copies ran while one was open for 3% of the time, Pallas kernels for 9%

profile of v2, /device:TPU:0, one launch (start us, length us, event | category | flops | bytes accessed | tf_op | source)
XLA Modules:
  0.0 365.5 jit_solution(12537642354301029816)
XLA Ops:
  7.2 1.3 fusion.47.gain_ref
  8.6 1.9 pack_weights.1
  12.2 1.0 fusion.36
  13.1 1.9 fusion.17.spread_ref
  15.0 119.1 %all-gather.2.cloned.1.call-done.big_ref = bf16[64,168,960]{2,1,0:T(8,128)(2,1)} async-done(((bf16[1,168,960]{2,1,0:T(8,128)(2,1)}), bf16[64,168,960]{2,1,0:T(8,128)(2,1)}) %all-gather.2.cloned.1.call-update) | async-done | bytes 20643856 | tf_op jit(solution)/shard_map/all_gather | solution.py:870
  134.1 0.9 slice_convert_fusion
  136.0 5.5 %slice.243 = bf16[64,40,960]{2,1,0:T(8,128)(2,1)} slice(bf16[64,168,960]{2,1,0:T(8,128)(2,1)} %all-gather.2.cloned.1.call-done.big_ref), slice={[0:64], [128:168], [0:960]} | slice | bytes 9830400 | tf_op jit(solution)/shard_map/slice | solution.py:871
  141.5 13.4 %layer_forward.2 = (bf16[128,960]{1,0:T(8,128)(2,1)}, bf16[8,128,128]{2,1,0:T(8,128)(2,1)}, bf16[3,128,128]{2,1,0:T(8,128)(2,1)}, bf16[3,128,128]{2,1,0:T(8,128)...) custom-call(bf16[128,960]{1,0:T(8,128)(2,1)} %bitcast.122, ...), custom_call_target="tpu_custom_call" | custom-call | flops 14300000256 | bytes 13000000 | tf_op jit(solution)/shard_map/layer_forward/pallas_call | solution.py:412
  154.9 2.2 collective-permute-start
  158.7 13.4 %layer_forward.3 = (bf16[128,960]{1,0:T(8,128)(2,1)}, bf16[8,128,128]{2,1,0:T(8,128)(2,1)}, bf16[3,128,128]{2,1,0:T(8,128)(2,1)}, bf16[3,128,128]{2,1,0:T(8,128)...) custom-call(bf16[128,960]{1,0:T(8,128)(2,1)} %broadcast_select_fusio, ...), custom_call_target="tpu_custom_call" | custom-call | flops 14300000256 | bytes 13000000 | tf_op jit(solution)/shard_map/layer_forward/pallas_call | solution.py:412
  172.2 14.1 %feed_forward_back.2 = (f32[128,960]{1,0:T(8,128)}, bf16[128,960]{1,0:T(8,128)(2,1)}, bf16[128,960]{1,0:T(8,128)(2,1)}, bf16[128,960]{1,0:T(8,128)(2,1)}, bf16[1...) custom-call(bf16[128,960]{1,0:T(8,128)(2,1)} %bitcast.123, ...), custom_call_target="tpu_custom_call" | custom-call | flops 15399999488 | bytes 14000000 | tf_op jit(solution)/shard_map/feed_forward_back/pallas_call | solution.py:434
  186.2 11.5 %attention_back.2 = (bf16[128,960]{1,0:T(8,128)(2,1)}, bf16[128,960]{1,0:T(8,128)(2,1)}, bf16[128,320]{1,0:T(8,128)(2,1)}, bf16[128,320]{1,0:T(8,128)(2,1)}, f32[1,960]{1,0:T(1,128)}, /*index=5*/bf16[128,960]{1,0:T(8,128)(2,1)}) custom-call(bf16[128,960]{1,0:T(8,128)(2,1)} %broadcast_select_fusion.1.x_ref, f32[128,960]{1,0:T(8,128)} %get-tuple-element.115.dm_ref, ...), custom_call_target="tpu_custom_call" | custom-call | flops 12650000384 | bytes 11500000 | tf_op jit(solution)/shard_map/attention_back/pallas_call | solution.py:454
  197.8 1.3 collective-permute-start.1
  199.1 2.8 fusion.14.mine_ref
  203.1 14.0 %feed_forward_back.3 = (f32[128,960]{1,0:T(8,128)}, bf16[128,960]{1,0:T(8,128)(2,1)}, bf16[128,960]{1,0:T(8,128)(2,1)}, bf16[128,960]{1,0:T(8,128)(2,1)}, bf16[1...) custom-call(bf16[128,960]{1,0:T(8,128)(2,1)} %broadcast_select_fusio, ...), custom_call_target="tpu_custom_call" | custom-call | flops 15399999488 | bytes 14000000 | tf_op jit(solution)/shard_map/feed_forward_back/pallas_call | solution.py:434
  217.2 6.6 %early_operands.1 = (bf16[1,32,16,128]{3,2,1,0:T(8,128)(2,1)}, bf16[1,32,16,128]{3,2,1,0:T(8,128)(2,1)}, bf16[2,32,16,128]{3,2,1,0:T(8,128)(2,1)}, bf16[2,32,16,...) custom-call(s32[64]{0:T(128)} %fusion.51.owner_ref, ...), custom_call_target="tpu_custom_call" | custom-call | flops 7699999744 | bytes 7000000 | tf_op jit(solution)/shard_map/early_operands/pallas_call | solution.py:595
  223.7 1.7 collective-permute-start.2
  225.4 1.3 collective-permute-start.3
  226.7 1.6 collective-permute-start.5
  228.3 2.1 collective-permute-start.4
  230.4 11.5 %attention_back.3 = (bf16[128,960]{1,0:T(8,128)(2,1)}, bf16[128,960]{1,0:T(8,128)(2,1)}, bf16[128,320]{1,0:T(8,128)(2,1)}, bf16[128,320]{1,0:T(8,128)(2,1)}, f32[1,960]{1,0:T(1,128)}, /*index=5*/bf16[128,960]{1,0:T(8,128)(2,1)}) custom-call(bf16[128,960]{1,0:T(8,128)(2,1)} %broadcast_select_fusion.1.x_ref, f32[128,960]{1,0:T(8,128)} %get-tuple-element.140.dm_ref, ...), custom_call_target="tpu_custom_call" | custom-call | flops 12650000384 | bytes 11500000 | tf_op jit(solution)/shard_map/attention_back/pallas_call | solution.py:454
  241.9 2.1 collective-permute-done.4.refs_4_
  244.4 1.5 collective-permute-done.3.refs_5_
  245.9 2.2 collective-permute-done.5.refs_5_
  248.2 4.1 %late_operands.1 = (bf16[2,32,16,128]{3,2,1,0:T(8,128)(2,1)}, bf16[2816,128]{1,0:T(8,128)(2,1)}) custom-call(bf16[1024,960]{1,0:T(8,128)(2,1)} %fusion.14.mine_ref, bf16[128,960]{1,0:T(8,128)(2,1)} %get-tuple-element.152.a_ref, f32[1,960]{1,0:T(1,128)} %get-tuple-element.153.attn_ref, f32[1,960]{1,0:T(1,128)} %get-tuple-element.154.ffn_ref, ...), custom_call_target="tpu_custom_call" | custom-call | flops 4400000000 | bytes 4000000 | tf_op jit(solution)/shard_map/late_operands/pallas_call | solution.py:613
  252.3 2.2 collective-permute-start.6
  254.5 7.2 %grad_products.4 = (bf16[16,16,16,128]{3,2,1,0:T(8,128)(2,1)}, bf16[16,16,16,128]{3,2,1,0:T(8,128)(2,1)}, bf16[12,16,16,128]{3,2,1,0:T(8,128)(2,1)}, bf16[12,16,16,128]{3,2,1,0:T(8,128)(2,1)}) custom-call(bf16[2,32,16,128]{3,2,1,0:T(8,128)(2,1)} %get-tuple-element.162.refs_0_, bf16[2,32,16,128]{3,2,1,0:T(8,128)(2,1)} %get-tuple-element.163.refs_1_, ...), custom_call_target="tpu_custom_call" | custom-call | flops 6160000000 | bytes 5600000 | tf_op jit(solution)/shard_map/grad_products/pallas_call | solution.py:705
  261.7 1.6 collective-permute-start.9
  263.4 1.1 collective-permute-start.10
  264.5 7.7 %grad_products.5 = (bf16[20,16,16,128]{3,2,1,0:T(8,128)(2,1)}, bf16[20,16,16,128]{3,2,1,0:T(8,128)(2,1)}, bf16[20,16,16,128]{3,2,1,0:T(8,128)(2,1)}, bf16[20,16,16,128]{3,2,1,0:T(8,128)(2,1)}) custom-call(bf16[1,32,16,128]{3,2,1,0:T(8,128)(2,1)} %get-tuple-element.174.refs_0_, bf16[1,32,16,128]{3,2,1,0:T(8,128)(2,1)} %get-tuple-element.175.refs_1_, ...), custom_call_target="tpu_custom_call" | custom-call | flops 8800000000 | bytes 8000000 | tf_op jit(solution)/shard_map/grad_products/pallas_call | solution.py:705
  272.2 1.7 collective-permute-start.14
  274.9 5.3 %grad_products.3 = (bf16[14,16,16,128]{3,2,1,0:T(8,128)(2,1)}, bf16[14,16,16,128]{3,2,1,0:T(8,128)(2,1)}) custom-call(bf16[2,32,16,128]{3,2,1,0:T(8,128)(2,1)} %get-tuple-element.158.refs_0_, bf16[2816,128]{1,0:T(8,128)(2,1)} %get-tuple-element.159.refs_1_, bf16[2816,128]{1,0:T(8,128)(2,1)} %copy-done.11), custom_call_target="tpu_custom_call" | custom-call | flops 3080000000 | bytes 2800000 | tf_op jit(solution)/shard_map/grad_products/pallas_call | solution.py:705
  280.2 1.6 collective-permute-start.7
  281.9 6.7 %collective-permute-done.10 = bf16[12,16,16,128]{3,2,1,0:T(8,128)(2,1)S(1)} collective-permute-done((bf16[12,16,16,128]{3,2,1,0:T(8,128)(2,1)}, bf16[12,16,16,128]{3,2,1,0:T(8,128)(2,1)S(1)}, u32[]{:S(2)}, u32[]{:S(2)}) %collective-permute-start.10) | collective-permute-done | bytes 786464 | tf_op jit(solution)/shard_map/ppermute | solution.py:723
  288.8 2.3 collective-permute-start.12
  291.4 2.2 collective-permute-start.11
  293.7 8.4 %collective-permute-done.14 = bf16[20,16,16,128]{3,2,1,0:T(8,128)(2,1)S(1)} collective-permute-done((bf16[20,16,16,128]{3,2,1,0:T(8,128)(2,1)}, bf16[20,16,16,128]{3,2,1,0:T(8,128)(2,1)S(1)}, u32[]{:S(2)}, u32[]{:S(2)}) %collective-permute-start.14) | collective-permute-done | bytes 1310752 | tf_op jit(solution)/shard_map/ppermute | solution.py:723
  302.1 1.5 collective-permute-done.15
  305.4 5.6 %collective-permute-done.12 = bf16[12,8,16,128]{3,2,0,1:T(8,128)(2,1)S(1)} collective-permute-done((bf16[12,8,16,128]{3,2,0,1:T(8,128)(2,1)S(1)}, bf16[12,8,16,128]{3,2,0,1:T(8,128)(2,1)S(1)}, u32[]{:S(2)}, u32[]{:S(2)}) %collective-permute-start.12) | collective-permute-done | bytes 393248 | tf_op jit(solution)/shard_map/ppermute | solution.py:723
  312.3 6.0 %collective-permute-done.17 = bf16[20,8,16,128]{3,2,0,1:T(8,128)(2,1)S(1)} collective-permute-done((bf16[20,8,16,128]{3,2,0,1:T(8,128)(2,1)S(1)}, bf16[20,8,16,128]{3,2,0,1:T(8,128)(2,1)S(1)}, u32[]{:S(2)}, u32[]{:S(2)}) %collective-permute-start.17) | collective-permute-done | bytes 655392 | tf_op jit(solution)/shard_map/ppermute | solution.py:723
  319.7 3.5 collective-permute-done.8
  323.6 2.1 collective-permute-start.18
  325.7 12.6 %collective-permute-done.18 = bf16[40,4,16,128]{3,2,0,1:T(8,128)(2,1)S(1)} collective-permute-done((bf16[40,4,16,128]{3,2,0,1:T(8,128)(2,1)S(1)}, bf16[40,4,16,128]{3,2,0,1:T(8,128)(2,1)S(1)}, u32[]{:S(2)}, u32[]{:S(2)}) %collective-permute-start.18) | collective-permute-done | bytes 655392 | tf_op jit(solution)/shard_map/ppermute | solution.py:723
  338.8 1.9 collective-permute-start.20
  340.7 6.5 %collective-permute-done.20 = bf16[40,2,16,128]{3,2,0,1:T(8,128)(2,1)S(1)} collective-permute-done((bf16[40,2,16,128]{3,2,0,1:T(8,128)(2,1)S(1)}, bf16[40,2,16,128]{3,2,0,1:T(8,128)(2,1)S(1)}, u32[]{:S(2)}, u32[]{:S(2)}) %collective-permute-start.20) | collective-permute-done | bytes 327712 | tf_op jit(solution)/shard_map/ppermute | solution.py:723
  348.7 1.2 collective-permute-start.22
  349.9 5.4 %collective-permute-done.22.came1_ref = bf16[40,1,16,128]{3,2,1,0:T(8,128)(2,1)S(1)} collective-permute-done((bf16[40,1,16,128]{3,2,1,0:T(8,128)(2,1)S(1)}, bf16[40,1,16,128]{3,2,1,0:T(8,128)(2,1)S(1)}, u32[]{:S(2)}, u32[]{:S(2)}) %collective-permute-start.22) | collective-permute-done | bytes 163872 | tf_op jit(solution)/shard_map/ppermute | solution.py:723
  356.0 2.2 weight_results.1
  (95 shorter events, 15.3 us)
Async XLA Ops:
  7.2 126.9 %all-gather.2.cloned.1.call-start = ((), (), s32[]{:S(2)}) async-start(), calls=%async_computation | async-start | bytes 22364160 | tf_op jit(solution)/shard_map/all_gather | solution.py:870
  8.6 1.9 copy-start.7
  141.5 16.5 %copy-start.5 = (bf16[2,64,960]{2,1,0:T(8,128)(2,1)S(1)}, bf16[2,64,960]{2,1,0:T(8,128)(2,1)}, u32[]{:S(2)}) copy-start(bf16[2,64,960]{2,1,0:T(8,128)(2,1)} %param.12) | copy-start | bytes 737284
  154.9 3.1 collective-permute-start
  186.2 16.1 %copy-start.6 = (bf16[2,64,960]{2,1,0:T(8,128)(2,1)S(1)}, bf16[2,64,960]{2,1,0:T(8,128)(2,1)}, u32[]{:S(2)}) copy-start(bf16[2,64,960]{2,1,0:T(8,128)(2,1)} %param.14) | copy-start | bytes 737284
  197.8 4.6 %collective-permute-start.1 = (bf16[128,960]{1,0:T(8,128)(2,1)}, bf16[128,960]{1,0:T(8,128)(2,1)S(1)}, u32[]{:S(2)}, u32[]{:S(2)}) collective-permute-start(bf16[128,960]{1,0:T(8,128)(2,1)} %get-tuple-element.121), channel_id=1, source_target_pairs={{64,0},{65,1},{66,2},{67,3},{68,4},{69,5},{70,6},{71,7},{72,8},{73... | collective-permute-start | bytes 737288 | tf_op jit(solution)/shard_map/ppermute | solution.py:888
  223.7 20.6 %collective-permute-start.2 = (bf16[3072,128]{1,0:T(8,128)(2,1)}, bf16[3072,128]{1,0:T(8,128)(2,1)S(1)}, u32[]{:S(2)}, u32[]{:S(2)}) collective-permute-start(bf16[3072,128]{1,0:T(8,128)(2,1)} %get-tuple-element.144.refs_2_), channel_id=1, source_target_pairs={{0,16},{1,17},{2,18},{3,19},{4,20},{5,21},{6,22},{7,23},{8,24},{9,... | collective-permute-start | bytes 2359304 | tf_op jit(solution)/shard_map/ppermute | solution.py:723
  225.4 20.5 %collective-permute-start.3 = (bf16[3072,128]{1,0:T(8,128)(2,1)}, bf16[3072,128]{1,0:T(8,128)(2,1)S(1)}, u32[]{:S(2)}, u32[]{:S(2)}) collective-permute-start(bf16[3072,128]{1,0:T(8,128)(2,1)} %get-tuple-element.145.refs_3_), channel_id=1, source_target_pairs={{0,4},{1,5},{2,6},{3,7},{4,0},{5,1},{6,2},{7,3},{8,12},{9,13},{10,... | collective-permute-start | bytes 2359304 | tf_op jit(solution)/shard_map/ppermute | solution.py:723
  226.7 21.4 %collective-permute-start.5 = (bf16[3072,128]{1,0:T(8,128)(2,1)}, bf16[3072,128]{1,0:T(8,128)(2,1)S(1)}, u32[]{:S(2)}, u32[]{:S(2)}) collective-permute-start(bf16[3072,128]{1,0:T(8,128)(2,1)} %get-tuple-element.147.refs_3_), channel_id=1, source_target_pairs={{0,3},{1,2},{2,1},{3,0},{4,7},{5,6},{6,5},{7,4},{8,11},{9,10},{10,... | collective-permute-start | bytes 2359304 | tf_op jit(solution)/shard_map/ppermute | solution.py:723
  228.3 15.7 %collective-permute-start.4 = (bf16[2048,128]{1,0:T(8,128)(2,1)}, bf16[2048,128]{1,0:T(8,128)(2,1)S(1)}, u32[]{:S(2)}, u32[]{:S(2)}) collective-permute-start(bf16[2048,128]{1,0:T(8,128)(2,1)} %get-tuple-element.146.refs_2_), channel_id=1, source_target_pairs={{0,12},{1,13},{2,14},{3,15},{4,8},{5,9},{6,10},{7,11},{8,4},{9,5},... | collective-permute-start | bytes 1572872 | tf_op jit(solution)/shard_map/ppermute | solution.py:723
  244.0 8.4 %copy-start.12 = (bf16[2048,128]{1,0:T(8,128)(2,1)}, bf16[2048,128]{1,0:T(8,128)(2,1)S(1)}, u32[]{:S(2)}) copy-start(bf16[2048,128]{1,0:T(8,128)(2,1)S(1)} %collective-permute-done.4.refs_4_) | copy-start | bytes 1572868
  244.4 7.9 %copy-start.8 = (bf16[3072,128]{1,0:T(8,128)(2,1)}, bf16[3072,128]{1,0:T(8,128)(2,1)S(1)}, u32[]{:S(2)}) copy-start(bf16[3072,128]{1,0:T(8,128)(2,1)S(1)} %collective-permute-done.2.refs_4_) | copy-start | bytes 2359300
  245.9 6.4 %copy-start.9 = (bf16[3072,128]{1,0:T(8,128)(2,1)}, bf16[3072,128]{1,0:T(8,128)(2,1)S(1)}, u32[]{:S(2)}) copy-start(bf16[3072,128]{1,0:T(8,128)(2,1)S(1)} %collective-permute-done.3.refs_5_) | copy-start | bytes 2359300
  248.2 4.2 %copy-start.10 = (bf16[3072,128]{1,0:T(8,128)(2,1)}, bf16[3072,128]{1,0:T(8,128)(2,1)S(1)}, u32[]{:S(2)}) copy-start(bf16[3072,128]{1,0:T(8,128)(2,1)S(1)} %collective-permute-done.5.refs_5_) | copy-start | bytes 2359300
  252.3 21.6 %collective-permute-start.6 = (bf16[2816,128]{1,0:T(8,128)(2,1)}, bf16[2816,128]{1,0:T(8,128)(2,1)S(1)}, u32[]{:S(2)}, u32[]{:S(2)}) collective-permute-start(bf16[2816,128]{1,0:T(8,128)(2,1)} %get-tuple-element.159.refs_1_), channel_id=1, source_target_pairs={{0,48},{1,49},{2,50},{3,51},{4,52},{5,53},{6,54},{7,55},{8,56},{9,... | collective-permute-start | bytes 2162696 | tf_op jit(solution)/shard_map/ppermute | solution.py:723
  261.7 26.8 %collective-permute-start.9 = (bf16[16,16,16,128]{3,2,1,0:T(8,128)(2,1)}, bf16[16,16,16,128]{3,2,1,0:T(8,128)(2,1)S(1)}, u32[]{:S(2)}, u32[]{:S(2)}) collective-permute-start(bf16[16,16,16,128]{3,2,1,0:T(8,128)(2,1)} %get-tuple-element.167), channel_id=1, source_target_pairs={{0,3},{1,2},{2,1},{3,0},{4,7},{5,6},{6,5},{7,4},{8,11},{9,10},{10,... | collective-permute-start | bytes 3145736 | tf_op jit(solution)/shard_map/ppermute | solution.py:723
  263.4 25.2 %collective-permute-start.10 = (bf16[12,16,16,128]{3,2,1,0:T(8,128)(2,1)}, bf16[12,16,16,128]{3,2,1,0:T(8,128)(2,1)S(1)}, u32[]{:S(2)}, u32[]{:S(2)}) collective-permute-start(bf16[12,16,16,128]{3,2,1,0:T(8,128)(2,1)} %get-tuple-element.168), channel_id=1, source_target_pairs={{0,48},{1,49},{2,50},{3,51},{4,52},{5,53},{6,54},{7,55},{8,56},{9,... | collective-permute-start | bytes 2359304 | tf_op jit(solution)/shard_map/ppermute | solution.py:723
  272.2 29.8 %collective-permute-start.14 = (bf16[20,16,16,128]{3,2,1,0:T(8,128)(2,1)}, bf16[20,16,16,128]{3,2,1,0:T(8,128)(2,1)S(1)}, u32[]{:S(2)}, u32[]{:S(2)}) collective-permute-start(bf16[20,16,16,128]{3,2,1,0:T(8,128)(2,1)} %get-tuple-element.179), channel_id=1, source_target_pairs={{0,4},{1,5},{2,6},{3,7},{4,0},{5,1},{6,2},{7,3},{8,12},{9,13},{10,... | collective-permute-start | bytes 3932168 | tf_op jit(solution)/shard_map/ppermute | solution.py:723
  274.0 29.6 %collective-permute-start.15 = (bf16[20,16,16,128]{3,2,1,0:T(8,128)(2,1)}, bf16[20,16,16,128]{3,2,1,0:T(8,128)(2,1)S(1)}, u32[]{:S(2)}, u32[]{:S(2)}) collective-permute-start(bf16[20,16,16,128]{3,2,1,0:T(8,128)(2,1)} %get-tuple-element.180), channel_id=1, source_target_pairs={{0,1},{1,0},{2,3},{3,2},{4,5},{5,4},{6,7},{7,6},{8,9},{9,8},{10,11... | collective-permute-start | bytes 3932168 | tf_op jit(solution)/shard_map/ppermute | solution.py:723
  274.0 0.9 copy-start.11
  274.9 13.7 %copy-start.4 = (bf16[12,16,16,128]{3,2,1,0:T(8,128)(2,1)S(1)}, bf16[12,16,16,128]{3,2,1,0:T(8,128)(2,1)}, u32[]{:S(2)}) copy-start(bf16[12,16,16,128]{3,2,1,0:T(8,128)(2,1)} %get-tuple-element.170) | copy-start | bytes 2359300
  274.9 16.1 %copy-start.2 = (bf16[16,16,16,128]{3,2,1,0:T(8,128)(2,1)S(1)}, bf16[16,16,16,128]{3,2,1,0:T(8,128)(2,1)}, u32[]{:S(2)}) copy-start(bf16[16,16,16,128]{3,2,1,0:T(8,128)(2,1)} %get-tuple-element.166) | copy-start | bytes 3145732
  280.2 23.3 %copy-start = (bf16[20,16,16,128]{3,2,1,0:T(8,128)(2,1)S(1)}, bf16[20,16,16,128]{3,2,1,0:T(8,128)(2,1)}, u32[]{:S(2)}) copy-start(bf16[20,16,16,128]{3,2,1,0:T(8,128)(2,1)} %get-tuple-element.182) | copy-start | bytes 3932164
  280.2 31.1 %collective-permute-start.7 = (bf16[14,16,16,128]{3,2,1,0:T(8,128)(2,1)}, bf16[14,16,16,128]{3,2,1,0:T(8,128)(2,1)S(1)}, u32[]{:S(2)}, u32[]{:S(2)}) collective-permute-start(bf16[14,16,16,128]{3,2,1,0:T(8,128)(2,1)} %get-tuple-element.161), channel_id=1, source_target_pairs={{0,12},{1,13},{2,14},{3,15},{4,8},{5,9},{6,10},{7,11},{8,4},{9,5},... | collective-permute-start | bytes 2752520 | tf_op jit(solution)/shard_map/ppermute | solution.py:723
  288.8 22.2 %collective-permute-start.12 = (bf16[12,8,16,128]{3,2,0,1:T(8,128)(2,1)S(1)}, bf16[12,8,16,128]{3,2,0,1:T(8,128)(2,1)S(1)}, u32[]{:S(2)}, u32[]{:S(2)}) collective-permute-start(bf16[12,8,16,128]{3,2,0,1:T(8,128)(2,1)S(1)} %copy.66), channel_id=1, source_target_pairs={{0,12},{1,13},{2,14},{3,15},{4,8},{5,9},{6,10},{7,11},{8,4},{9,5},... | collective-permute-start | bytes 1179656 | tf_op jit(solution)/shard_map/ppermute | solution.py:723
  291.0 13.0 %copy-start.1 = (bf16[20,16,16,128]{3,2,1,0:T(8,128)(2,1)S(1)}, bf16[20,16,16,128]{3,2,1,0:T(8,128)(2,1)}, u32[]{:S(2)}) copy-start(bf16[20,16,16,128]{3,2,1,0:T(8,128)(2,1)} %get-tuple-element.178) | copy-start | bytes 3932164
  291.4 19.6 %collective-permute-start.11 = (bf16[16,8,16,128]{3,2,1,0:T(8,128)(2,1)S(1)}, bf16[16,8,16,128]{3,2,1,0:T(8,128)(2,1)S(1)}, u32[]{:S(2)}, u32[]{:S(2)}) collective-permute-start(bf16[16,8,16,128]{3,2,1,0:T(8,128)(2,1)S(1)} %get-tuple-element.204), channel_id=1, source_target_pairs={{0,48},{1,49},{2,50},{3,51},{4,52},{5,53},{6,54},{7,55},{8,56},{9,... | collective-permute-start | bytes 1572872 | tf_op jit(solution)/shard_map/ppermute | solution.py:723
  303.9 14.5 %collective-permute-start.17 = (bf16[20,8,16,128]{3,2,0,1:T(8,128)(2,1)S(1)}, bf16[20,8,16,128]{3,2,0,1:T(8,128)(2,1)S(1)}, u32[]{:S(2)}, u32[]{:S(2)}) collective-permute-start(bf16[20,8,16,128]{3,2,0,1:T(8,128)(2,1)S(1)} %copy.71), channel_id=1, source_target_pairs={{0,16},{1,17},{2,18},{3,19},{4,20},{5,21},{6,22},{7,23},{8,24},{9,... | collective-permute-start | bytes 1966088 | tf_op jit(solution)/shard_map/ppermute | solution.py:723
  304.4 6.9 %copy-start.3 = (bf16[14,16,16,128]{3,2,1,0:T(8,128)(2,1)S(1)}, bf16[14,16,16,128]{3,2,1,0:T(8,128)(2,1)}, u32[]{:S(2)}) copy-start(bf16[14,16,16,128]{3,2,1,0:T(8,128)(2,1)} %get-tuple-element.160) | copy-start | bytes 2752516
  304.4 14.7 %collective-permute-start.16 = (bf16[20,8,16,128]{3,2,1,0:T(8,128)(2,1)S(1)}, bf16[20,8,16,128]{3,2,1,0:T(8,128)(2,1)S(1)}, u32[]{:S(2)}, u32[]{:S(2)}) collective-permute-start(bf16[20,8,16,128]{3,2,1,0:T(8,128)(2,1)S(1)} %get-tuple-element.202), channel_id=1, source_target_pairs={{0,1},{1,0},{2,3},{3,2},{4,5},{5,4},{6,7},{7,6},{8,9},{9,8},{10,11... | collective-permute-start | bytes 1966088 | tf_op jit(solution)/shard_map/ppermute | solution.py:723
  311.7 11.5 %collective-permute-start.8 = (bf16[14,8,16,128]{3,2,0,1:T(8,128)(2,1)S(1)}, bf16[14,8,16,128]{3,2,0,1:T(8,128)(2,1)S(1)}, u32[]{:S(2)}, u32[]{:S(2)}) collective-permute-start(bf16[14,8,16,128]{3,2,0,1:T(8,128)(2,1)S(1)} %copy.64), channel_id=1, source_target_pairs={{0,3},{1,2},{2,1},{3,0},{4,7},{5,6},{6,5},{7,4},{8,11},{9,10},{10,... | collective-permute-start | bytes 1376264 | tf_op jit(solution)/shard_map/ppermute | solution.py:723
  323.3 15.0 %collective-permute-start.13 = (bf16[42,4,16,128]{3,2,0,1:T(8,128)(2,1)S(1)}, bf16[42,4,16,128]{3,2,0,1:T(8,128)(2,1)S(1)}, u32[]{:S(2)}, u32[]{:S(2)}) collective-permute-start(bf16[42,4,16,128]{3,2,0,1:T(8,128)(2,1)S(1)} %pad_maximum_fusion.1), channel_id=1, source_target_pairs={{0,16},{1,17},{2,18},{3,19},{4,20},{5,21},{6,22},{7,23},{8,24},{9,... | collective-permute-start | bytes 2064392 | tf_op jit(solution)/shard_map/ppermute | solution.py:723
  323.6 14.8 %collective-permute-start.18 = (bf16[40,4,16,128]{3,2,0,1:T(8,128)(2,1)S(1)}, bf16[40,4,16,128]{3,2,0,1:T(8,128)(2,1)S(1)}, u32[]{:S(2)}, u32[]{:S(2)}) collective-permute-start(bf16[40,4,16,128]{3,2,0,1:T(8,128)(2,1)S(1)} %pad_maximum_fusion.2), channel_id=1, source_target_pairs={{0,48},{1,49},{2,50},{3,51},{4,52},{5,53},{6,54},{7,55},{8,56},{9,... | collective-permute-start | bytes 1966088 | tf_op jit(solution)/shard_map/ppermute | solution.py:723
  338.5 8.6 %collective-permute-start.19 = (bf16[42,2,16,128]{3,2,0,1:T(8,128)(2,1)S(1)}, bf16[42,2,16,128]{3,2,0,1:T(8,128)(2,1)S(1)}, u32[]{:S(2)}, u32[]{:S(2)}) collective-permute-start(bf16[42,2,16,128]{3,2,0,1:T(8,128)(2,1)S(1)} %get-tuple-element.208), channel_id=1, source_target_pairs={{0,4},{1,5},{2,6},{3,7},{4,0},{5,1},{6,2},{7,3},{8,12},{9,13},{10,... | collective-permute-start | bytes 1032200 | tf_op jit(solution)/shard_map/ppermute | solution.py:723
  338.8 8.4 %collective-permute-start.20 = (bf16[40,2,16,128]{3,2,0,1:T(8,128)(2,1)S(1)}, bf16[40,2,16,128]{3,2,0,1:T(8,128)(2,1)S(1)}, u32[]{:S(2)}, u32[]{:S(2)}) collective-permute-start(bf16[40,2,16,128]{3,2,0,1:T(8,128)(2,1)S(1)} %get-tuple-element.210), channel_id=1, source_target_pairs={{0,12},{1,13},{2,14},{3,15},{4,8},{5,9},{6,10},{7,11},{8,4},{9,5},... | collective-permute-start | bytes 983048 | tf_op jit(solution)/shard_map/ppermute | solution.py:723
  347.9 7.3 %collective-permute-start.21 = (bf16[42,1,16,128]{3,2,1,0:T(8,128)(2,1)S(1)}, bf16[42,1,16,128]{3,2,1,0:T(8,128)(2,1)S(1)}, u32[]{:S(2)}, u32[]{:S(2)}) collective-permute-start(bf16[42,1,16,128]{3,2,1,0:T(8,128)(2,1)S(1)} %get-tuple-element.221), channel_id=1, source_target_pairs={{0,1},{1,0},{2,3},{3,2},{4,5},{5,4},{6,7},{7,6},{8,9},{9,8},{10,11... | collective-permute-start | bytes 516104 | tf_op jit(solution)/shard_map/ppermute | solution.py:723
  348.7 6.5 %collective-permute-start.22 = (bf16[40,1,16,128]{3,2,1,0:T(8,128)(2,1)S(1)}, bf16[40,1,16,128]{3,2,1,0:T(8,128)(2,1)S(1)}, u32[]{:S(2)}, u32[]{:S(2)}) collective-permute-start(bf16[40,1,16,128]{3,2,1,0:T(8,128)(2,1)S(1)} %get-tuple-element.223), channel_id=1, source_target_pairs={{0,3},{1,2},{2,1},{3,0},{4,7},{5,6},{6,5},{7,4},{8,11},{9,10},{10,... | collective-permute-start | bytes 491528 | tf_op jit(solution)/shard_map/ppermute | solution.py:723
  355.2 0.7 copy-start.14
  355.2 0.8 copy-start.13
Sparse Core Ops, SparseCore 0:
  10.8 123.2 all-gather.1
